TPU v7x, 32 devices: a whole 2x2x4 slice. The times are simulated.
32 devices in a mesh: rep: 4 (over y, x), row: 8 (over z, core).
Axes of the slice: x: 2, y: 2, z: 4, core: 2. Of those that a mesh axis runs over, the one named last changes fastest.
Arguments:
- node_feat: float32 [4096, 256], P(('rep', 'row')), may hold values from -6 to 6
- weight: float32 [256, 256], replicated, may hold values from -0.375 to 0.375
- bias: float32 [256], replicated, may hold values from -0.5 to 0.5
- cotangent: float32 [4096, 256], P(('rep', 'row')), may hold values from -6 to 6
- blocks: float32 [4, 8, 64, 4096], P('rep', 'row'), may hold values from -0.1875 to 0.1875
- row_block: int32 [4, 8, 64], P('rep', 'row'), may hold values from 0 to 7
- col_block: int32 [4, 8, 64], P('rep', 'row'), may hold values from 0 to 3
- live_blocks: int32 [4, 8], P('rep', 'row'), may hold values from 12 to 64, as said below
- send_list: int32 [4, 2048], P('rep'), may hold values from 0 to 127
Outputs:
- activated: float32 [4096, 256], P(('rep', 'row'))
- feat_grad: float32 [4096, 256], P(('rep', 'row'))
- weight_grad: float32 [256, 256], replicated
- bias_grad: float32 [256], replicated
Inputs may be any that keep to these rules, and one draw needn't show every extreme that they name: `live_blocks`: each value is 64 divided by a whole number from 1 to 5, rounded down; some device has all 64 slots used.
All inputs are finite; a program needn't handle non-finite values.
Results may differ from a plain program's by a relative error of at most 0.0001.
Values sent between devices are 32-bit elements; how exact they have to be, the bound alone decides.
No kernel may reach another device: no remote copies, remote signals or barrier semaphores. Data moves between devices by JAX's collectives and lax.ppermute only.
A program may use at most 64 MiB of HBM per device.

v0:
```python
import functools

import jax
import jax.numpy as jnp
from jax import lax
from jax.experimental import pallas as pl
from jax.experimental.pallas import tpu as pltpu
from jax.sharding import PartitionSpec as P


BS = 64
LANES = 128
PAD = 8
FLOOR = 16 * 2**20
F32 = jnp.float32
BF16 = jnp.bfloat16
NN = (((1,), (0,)), ((), ()))
TN = (((0,), (0,)), ((), ()))
NT = (((1,), (1,)), ((), ()))


def split(x):
    high = x.astype(BF16)
    return high, (x - high.astype(F32)).astype(BF16)


def mm(a, b, dims):
    return lax.dot_general(a, b, dims, preferred_element_type=F32)


def mm3(a, b, dims):
    return mm(a[0], b[0], dims) + (mm(a[0], b[1], dims) + mm(a[1], b[0], dims))


def call(kernel, outs, args, scratch=(), flops=0, smem=(), hbm=()):
    out_bytes = sum(int(o.size) * o.dtype.itemsize for o in outs)
    in_bytes = sum(int(a.size) * a.dtype.itemsize for a in args)
    limit = max(FLOOR, 4 * (in_bytes + out_bytes))
    return pl.pallas_call(
        kernel,
        out_shape=outs,
        in_specs=[
            pl.BlockSpec(
                memory_space=pltpu.SMEM if k in smem else pltpu.HBM if k in hbm else pltpu.VMEM
            )
            for k in range(len(args))
        ],
        out_specs=[pl.BlockSpec(memory_space=pltpu.VMEM) for _ in outs],
        scratch_shapes=list(scratch),
        cost_estimate=pl.CostEstimate(
            flops=flops, transcendentals=0, bytes_accessed=in_bytes + out_bytes
        ),
        compiler_params=pltpu.CompilerParams(vmem_limit_bytes=limit),
    )(*args)


def rows_at(index, count):
    return pl.ds(pl.multiple_of(index * count, count), count)


def one_hot(wanted, nodes):
    node = lax.broadcasted_iota(jnp.int32, (nodes, wanted.shape[1]), 0)
    return (node == wanted).astype(BF16)


def tree_sum(terms):
    terms = list(terms)
    while len(terms) > 1:
        terms = [terms[k] + terms[k + 1] for k in range(0, len(terms), 2)]
    return terms[0]


def put_pairs(outs, buffer, me, per):
    for pair, out in enumerate(outs):
        for core in range(2):
            source = rows_at(lax.bitwise_xor(me, 2 * pair + core), per)
            out[core * per : (core + 1) * per, :] = buffer[source, :]


def take_pairs(own_ref, partner_ref, buffer, me, per):
    for pair in range(buffer.shape[0] // (2 * per)):
        rows = slice(pair * per, (pair + 1) * per)
        buffer[rows_at(lax.bitwise_xor(me, 2 * pair), per), :] = own_ref[rows, :]
        buffer[rows_at(lax.bitwise_xor(me, 2 * pair + 1), per), :] = partner_ref[rows, :]


def gather_rows(list_hbm, feat_hbm, *refs):
    outs, wanted_ref, feat_ref, buffer, sems = refs[:-4], refs[-4], refs[-3], refs[-2], refs[-1]
    me = lax.axis_index("row")
    slots = buffer.shape[0]
    copies = [
        pltpu.make_async_copy(feat_hbm, feat_ref, sems.at[0]),
        pltpu.make_async_copy(list_hbm.at[:, rows_at(me, slots)], wanted_ref, sems.at[1]),
    ]
    for copy in copies:
        copy.start()
    copies[1].wait()
    pick = one_hot(wanted_ref[...], feat_ref.shape[0]).T
    copies[0].wait()
    high, low = split(feat_ref[...])
    buffer[...] = mm(pick, high, NN) + mm(pick, low, NN)
    put_pairs(outs, buffer, me, outs[0].shape[0] // 2)


def aggregate(pairs, high_ref, low_ref, own_ref, partner_ref, *outs):
    per = own_ref.shape[0] // pairs
    same = lax.axis_index("row") % 2 == 0
    own, partner = own_ref[...], partner_ref[...]
    lower, upper = jnp.where(same, own, partner), jnp.where(same, partner, own)
    pieces = []
    for pair in range(pairs):
        for half in (lower, upper):
            pieces.append(half[pair * per : (pair + 1) * per, :])
    border = jnp.concatenate(pieces, axis=0)
    result = mm3((high_ref[...], low_ref[...]), split(border), NN)
    for s, out in enumerate(outs):
        out[...] = result[s * out.shape[0] : (s + 1) * out.shape[0], :]


def activate(groups, members, *refs):
    pieces = refs[:groups]
    high_ref, low_ref, bias_ref, cot_ref, pre_ref, grad_ref, keep_ref, send_ref, buffer = refs[groups:]
    me = lax.axis_index("row")
    total = tree_sum([piece[...] for piece in pieces])
    total_split = split(total)
    pre = mm3(total_split, (high_ref[...], low_ref[...]), NN) + bias_ref[...]
    gate = jax.nn.sigmoid(pre)
    pre_ref[...] = pre
    grad = cot_ref[...] * (gate * (1.0 + pre * (1.0 - gate)))
    grad_ref[...] = grad
    buffer[...] = mm3(total_split, split(grad), TN)
    chunk = buffer.shape[0] // members
    sums = jnp.broadcast_to(jnp.sum(grad, axis=0, keepdims=True), (PAD, grad.shape[1]))
    for s in range(members):
        target = send_ref if s % 2 else keep_ref
        start = (s // 2) * (chunk + PAD)
        target[start : start + chunk, :] = buffer[rows_at(lax.bitwise_xor(me, s), chunk), :]
        target[start + chunk : start + chunk + PAD, :] = sums


def spread(groups, high_ref, low_ref, *refs):
    pieces, outs = refs[:groups], refs[groups:]
    grads = jnp.concatenate([piece[...] for piece in pieces], axis=0)
    result = mm3((high_ref[...], low_ref[...]), split(grads), NN)
    same = lax.axis_index("row") % 2 == 0
    per = outs[0].shape[0] // 2
    for pair, out in enumerate(outs):
        lower = result[2 * pair * per : (2 * pair + 1) * per, :]
        upper = result[(2 * pair + 1) * per : (2 * pair + 2) * per, :]
        out[0:per, :] = jnp.where(same, lower, upper)
        out[per : 2 * per, :] = jnp.where(same, upper, lower)


def collect(per, wanted_ref, high_ref, low_ref, own_ref, partner_ref, out_ref, border):
    me = lax.axis_index("row")
    take_pairs(own_ref, partner_ref, border, me, per)
    pick = one_hot(wanted_ref[...], out_ref.shape[0])
    high, low = split(border[...])
    proj = mm(pick, high, NN) + mm(pick, low, NN)
    out_ref[...] = mm3(split(proj), (high_ref[...], low_ref[...]), NT)


def finish(members, summed_ref, own_ref, partner_ref, weight_ref, bias_ref):
    me = lax.axis_index("row")
    chunk = weight_ref.shape[0] // members
    for s in range(members):
        piece = partner_ref if s % 2 else own_ref
        start = (s // 2) * chunk
        weight_ref[rows_at(lax.bitwise_xor(me, s), chunk), :] = piece[start : start + chunk, :]
    bias_ref[...] = summed_ref[chunk : chunk + 1, :]


def emit(pre_ref, act_ref):
    pre = pre_ref[...]
    act_ref[...] = pre * jax.nn.sigmoid(pre)


def exchange(value, axis, shift):
    size = lax.axis_size(axis)
    return lax.ppermute(value, axis, [(i, i ^ shift) for i in range(size)])


def swap_rows(sends):
    pieces = [sends[0]]
    pieces += [exchange(sends[p], "row", 2 * p) for p in range(1, len(sends))]
    per = sends[0].shape[0] // 2
    own = jnp.concatenate([piece[:per] for piece in pieces], axis=0)
    partner = jnp.concatenate([piece[per:] for piece in pieces], axis=0)
    return [own, exchange(partner, "row", 1)]


def layer(
    node_feat, weight, bias, cotangent, blocks, row_block, col_block, live_blocks, send_list
):
    nodes, width = node_feat.shape
    groups, members = lax.axis_size("rep"), lax.axis_size("row")
    capacity = blocks.shape[2]
    per = send_list.shape[-1] // (members * members)
    slots = members * per
    row_blocks = groups * nodes // BS
    col_blocks = slots // BS
    rows = row_blocks * BS
    assert 2 * per == BS and nodes % BS == 0
    pairs = members // 2
    shape = lambda n: jax.ShapeDtypeStruct((n, width), F32)
    vmem = lambda n: pltpu.VMEM((n, width), F32)

    *sends, wanted = call(
        gather_rows,
        [shape(2 * per)] * pairs + [jax.ShapeDtypeStruct((1, slots), jnp.int32)],
        [pltpu.with_memory_space_constraint(x, pltpu.HBM) for x in (send_list, node_feat)],
        [vmem(nodes), vmem(slots), pltpu.SemaphoreType.DMA((2,))],
        hbm=(0, 1),
    )
    border = swap_rows(sends)
    wide = jax.ShapeDtypeStruct((rows, slots), BF16)
    tall = jax.ShapeDtypeStruct((slots, rows), BF16)
    bias_row = jax.ShapeDtypeStruct((1, width), F32)
    dense = call(
        functools.partial(build, nodes // BS),
        [wide, wide],
        [
            live_blocks,
            *(
                pltpu.with_memory_space_constraint(x, pltpu.HBM)
                for x in (row_block[0], col_block[0], blocks[0, 0])
            ),
        ],
        [
            pltpu.VMEM((1, capacity), jnp.int32),
            pltpu.VMEM((1, capacity), jnp.int32),
            pltpu.VMEM((capacity, BS * BS), F32),
            pltpu.VMEM((slots // LANES, rows, LANES), F32),
            pltpu.SemaphoreType.DMA((3,)),
        ],
        flops=4 * row_blocks * col_blocks * capacity * BS * BS,
        hbm=(1, 2, 3),
    )
    partials = call(
        functools.partial(aggregate, pairs),
        [shape(nodes)] * groups,
        [*dense, *border],
        flops=6 * rows * slots * width,
    )
    half_weight = jax.ShapeDtypeStruct(weight.shape, BF16)
    *turned, bias_here, weight_high, weight_low = call(
        prepare, [tall, tall, bias_row, half_weight, half_weight], [*dense, bias[None, :], weight]
    )
    parts = [partials[0]] + [exchange(partials[s], "rep", s) for s in range(1, groups)]
    chunk = width // members
    padded = pairs * (chunk + PAD)
    pre, grad, keep, send = call(
        functools.partial(activate, groups, members),
        [shape(nodes), shape(nodes), shape(padded), shape(padded)],
        parts + [weight_high, weight_low, bias_here, cotangent],
        [vmem(width)],
        flops=12 * nodes * width * width,
    )
    (activated,) = call(emit, [shape(nodes)], [pre])
    grads = [grad] + [exchange(grad, "rep", s) for s in range(1, groups)]
    backs = call(
        functools.partial(spread, groups),
        [shape(2 * per)] * pairs,
        turned + grads,
        flops=6 * rows * slots * width,
    )
    returned = swap_rows(backs)
    (feat_grad,) = call(
        functools.partial(collect, per),
        [shape(nodes)],
        [wanted, weight_high, weight_low] + returned,
        [vmem(slots)],
        flops=6 * nodes * width * width,
    )
    total = keep + exchange(send, "row", 1)
    size = chunk + PAD
    owned = [total[p * size : (p + 1) * size] for p in range(pairs)]
    owned[1:] = [exchange(owned[p], "row", 2 * p) for p in range(1, pairs)]
    part = tree_sum(owned)
    summed = tree_sum([part] + [exchange(part, "rep", s) for s in range(1, groups)])
    done = summed[:chunk]
    chunks = [done] + [exchange(done, "row", 2 * p) for p in range(1, pairs)]
    own = jnp.concatenate(chunks, axis=0)
    partner = exchange(own, "row", 1)
    weight_grad, bias_grad = call(
        functools.partial(finish, members),
        [shape(width), shape(1)],
        [summed, own, partner],
    )
    return (activated, feat_grad, weight_grad, bias_grad[0])


def build(shard_blocks, live_ref, rows_hbm, cols_hbm, blocks_hbm, high_ref, low_ref, *refs):
    rows_ref, cols_ref, blocks_ref, dense, sems = refs
    copies = [
        pltpu.make_async_copy(blocks_hbm, blocks_ref, sems.at[0]),
        pltpu.make_async_copy(rows_hbm, rows_ref, sems.at[1]),
        pltpu.make_async_copy(cols_hbm, cols_ref, sems.at[2]),
    ]
    for copy in copies:
        copy.start()
    for copy in copies[1:]:
        copy.wait()
    row_blocks = high_ref.shape[0] // BS
    col_blocks = high_ref.shape[1] // BS
    capacity = blocks_ref.shape[0]
    pairs = row_blocks * col_blocks
    me, group = lax.axis_index("row"), lax.axis_index("rep")
    rows = lax.bitwise_xor(rows_ref[...], group * shard_blocks)
    cols = lax.bitwise_xor(cols_ref[...], me // 2)
    pair = lax.broadcasted_iota(jnp.int32, (pairs, capacity), 0)
    slot = lax.broadcasted_iota(jnp.int32, (pairs, capacity), 1)
    pick = ((pair == cols * row_blocks + rows) & (slot < live_ref[...])).astype(BF16)
    copies[0].wait()
    high, low = split(blocks_ref[...])
    product = mm(pick, high, NN) + mm(pick, low, NN)
    left = lax.broadcasted_iota(jnp.int32, (row_blocks, LANES), 1) < BS
    for t in range(blocks_ref.shape[1] // LANES):
        lanes = slice(t * LANES, (t + 1) * LANES)
        for u in range(col_blocks // 2):
            first = product[2 * u * row_blocks : (2 * u + 1) * row_blocks, lanes]
            second = product[(2 * u + 1) * row_blocks : (2 * u + 2) * row_blocks, lanes]
            even = jnp.where(left, first, pltpu.roll(second, BS, 1))
            odd = jnp.where(left, pltpu.roll(first, BS, 1), second)
            for parity, value in ((0, even), (1, odd)):
                dense[u, pl.ds(2 * t + parity, row_blocks, stride=BS), :] = value
    for u in range(col_blocks // 2):
        lanes = slice(u * LANES, (u + 1) * LANES)
        high_ref[:, lanes], low_ref[:, lanes] = split(dense[u])


def prepare(high_ref, low_ref, bias_ref, weight_ref, *refs):
    high_t_ref, low_t_ref, bias_out, weight_high, weight_low = refs
    high_t_ref[...] = high_ref[...].astype(F32).T.astype(BF16)
    low_t_ref[...] = low_ref[...].astype(F32).T.astype(BF16)
    bias_out[...] = bias_ref[...]
    weight_high[...], weight_low[...] = split(weight_ref[...])


def solution(mesh):
    return sharded(mesh)


def sharded(mesh):
    return jax.shard_map(
        layer,
        mesh=mesh,
        in_specs=(
            P(("rep", "row"), None),
            P(),
            P(),
            P(("rep", "row"), None),
            P("rep", "row", None, None),
            P("rep", "row", None),
            P("rep", "row", None),
            P("rep", "row"),
            P("rep", None),
        ),
        out_specs=(P(("rep", "row"), None), P(("rep", "row"), None), P(), P()),
        check_vma=False,
    )
```

profile of v0, /device:TPU:0, one launch (start us, length us, event | category | flops | bytes accessed | tf_op | source)
XLA Modules:
  0.0 67.6 jit_solution(4564900177711724665)
XLA Ops:
  0.6 1.2 %shard_map.121 = (f32[64,256]{1,0:T(8,128)S(1)}, f32[64,256]{1,0:T(8,128)S(1)}, f32[64,256]{1,0:T(8,128)S(1)}, f32[64,256]{1,0:T(8,128)S(1)}, s32[1,256]{1,0:T(1,128)S(1)}) custom-call(s32[1,2048]{1,0:T(1,128)} %list_hbm.1, f32[128,256]{1,0:T(8,128)} %feat_hbm.1), custom_call_target="tpu_custom_call" | custom-call | bytes 402432 | tf_op jit(solution)/shard_map/pallas_call | solution.py:39
  1.8 3.1 %collective-permute-start = (f32[64,256]{1,0:T(8,128)S(1)}, f32[64,256]{1,0:T(8,128)S(1)}, u32[]{:S(2)}, u32[]{:S(2)}) collective-permute-start(f32[64,256]{1,0:T(8,128)S(1)} %get-tuple-element.33), channel_id=1, source_target_pairs={{0,2},{1,3},{2,0},{3,1},{4,6},{5,7},{6,4},{7,5},{8,10},{9,11},{10,... | collective-permute-start | bytes 196616 | tf_op jit(solution)/shard_map/ppermute | solution.py:180
  4.9 2.6 %collective-permute-start.1 = (f32[64,256]{1,0:T(8,128)S(1)}, f32[64,256]{1,0:T(8,128)S(1)}, u32[]{:S(2)}, u32[]{:S(2)}) collective-permute-start(f32[64,256]{1,0:T(8,128)S(1)} %get-tuple-element.34), channel_id=1, source_target_pairs={{0,4},{1,5},{2,6},{3,7},{4,0},{5,1},{6,2},{7,3},{8,12},{9,13},{10,... | collective-permute-start | bytes 196616 | tf_op jit(solution)/shard_map/ppermute | solution.py:180
  7.5 0.0 collective-permute-start.2
  7.5 0.0 collective-permute-done
  7.5 4.6 %collective-permute-done.1 = f32[64,256]{1,0:T(8,128)S(1)} collective-permute-done((f32[64,256]{1,0:T(8,128)S(1)}, f32[64,256]{1,0:T(8,128)S(1)}, u32[]{:S(2)}, u32[]{:S(2)}) %collective-permute-start.1) | collective-permute-done | bytes 65568 | tf_op jit(solution)/shard_map/ppermute | solution.py:180
  12.2 1.4 %collective-permute-done.2 = f32[64,256]{1,0:T(8,128)S(1)} collective-permute-done((f32[64,256]{1,0:T(8,128)S(1)}, f32[64,256]{1,0:T(8,128)S(1)}, u32[]{:S(2)}, u32[]{:S(2)}) %collective-permute-start.2) | collective-permute-done | bytes 65568 | tf_op jit(solution)/shard_map/ppermute | solution.py:180
  13.6 0.1 collective-permute-start.3
  14.3 2.0 %shard_map.120 = (bf16[512,256]{1,0:T(8,128)(2,1)S(1)}, bf16[512,256]{1,0:T(8,128)(2,1)S(1)}) custom-call(s32[1,1]{1,0:T(1,128)S(6)} %copy.13.live_ref, s32[1,64]{1,0:T(1,128)} %bitcast.7, s32[1,64]{1,0:T(1,128)} %bitcast.8, f32[64,4096]{1,0:T(8,128)} %bitcast.6), custom_call_target="tpu_custom_call" | custom-call | flops 33554432 | bytes 1573380 | tf_op jit(solution)/shard_map/pallas_call | solution.py:39
  16.4 0.0 collective-permute-done.3.partner_ref
  16.4 0.0 copy-start
  16.4 0.4 shard_map.122
  16.8 1.6 %collective-permute-start.4 = (f32[128,256]{1,0:T(8,128)S(1)}, f32[128,256]{1,0:T(8,128)S(1)}, u32[]{:S(2)}, u32[]{:S(2)}) collective-permute-start(f32[128,256]{1,0:T(8,128)S(1)} %get-tuple-element.37), channel_id=1, source_target_pairs={{0,8},{8,0},{16,24},{24,16},{1,9},{9,1},{17,25},{25,17},{2,10},{10... | collective-permute-start | bytes 393224 | tf_op jit(solution)/shard_map/ppermute | solution.py:180
  18.3 1.5 %collective-permute-start.5 = (f32[128,256]{1,0:T(8,128)S(1)}, f32[128,256]{1,0:T(8,128)S(1)}, u32[]{:S(2)}, u32[]{:S(2)}) collective-permute-start(f32[128,256]{1,0:T(8,128)S(1)} %get-tuple-element.38), channel_id=1, source_target_pairs={{0,16},{8,24},{16,0},{24,8},{1,17},{9,25},{17,1},{25,9},{2,18},{10... | collective-permute-start | bytes 393224 | tf_op jit(solution)/shard_map/ppermute | solution.py:180
  19.9 0.5 collective-permute-start.6
  20.3 0.0 copy-done
  20.3 0.2 copy-done.2
  20.5 0.0 copy-start.1
  20.5 0.2 shard_map.123
  20.8 2.4 %collective-permute-done.4.refs_1_ = f32[128,256]{1,0:T(8,128)S(1)} collective-permute-done((f32[128,256]{1,0:T(8,128)S(1)}, f32[128,256]{1,0:T(8,128)S(1)}, u32[]{:S(2)}, u32[]{:S(2)}) %collective-permute-start.4) | collective-permute-done | bytes 131104 | tf_op jit(solution)/shard_map/ppermute | solution.py:180
  23.2 3.6 %collective-permute-done.5.refs_2_ = f32[128,256]{1,0:T(8,128)S(1)} collective-permute-done((f32[128,256]{1,0:T(8,128)S(1)}, f32[128,256]{1,0:T(8,128)S(1)}, u32[]{:S(2)}, u32[]{:S(2)}) %collective-permute-start.5) | collective-permute-done | bytes 131104 | tf_op jit(solution)/shard_map/ppermute | solution.py:180
  26.8 0.0 collective-permute-done.6.refs_3_
  26.8 0.0 copy-done.1
  26.8 0.6 shard_map.124
  27.4 1.3 %collective-permute-start.7 = (f32[128,256]{1,0:T(8,128)S(1)}, f32[128,256]{1,0:T(8,128)S(1)}, u32[]{:S(2)}, u32[]{:S(2)}) collective-permute-start(f32[128,256]{1,0:T(8,128)S(1)} %get-tuple-element.47.refs_0_), channel_id=1, source_target_pairs={{0,8},{8,0},{16,24},{24,16},{1,9},{9,1},{17,25},{25,17},{2,10},{10... | collective-permute-start | bytes 393224 | tf_op jit(solution)/shard_map/ppermute | solution.py:180
  28.7 0.8 %collective-permute-start.8 = (f32[128,256]{1,0:T(8,128)S(1)}, f32[128,256]{1,0:T(8,128)S(1)}, u32[]{:S(2)}, u32[]{:S(2)}) collective-permute-start(f32[128,256]{1,0:T(8,128)S(1)} %get-tuple-element.47.refs_0_), channel_id=1, source_target_pairs={{0,16},{8,24},{16,0},{24,8},{1,17},{9,25},{17,1},{25,9},{2,18},{10... | collective-permute-start | bytes 393224 | tf_op jit(solution)/shard_map/ppermute | solution.py:180
  29.5 1.4 %collective-permute-start.9 = (f32[128,256]{1,0:T(8,128)S(1)}, f32[128,256]{1,0:T(8,128)S(1)}, u32[]{:S(2)}, u32[]{:S(2)}) collective-permute-start(f32[128,256]{1,0:T(8,128)S(1)} %get-tuple-element.47.refs_0_), channel_id=1, source_target_pairs={{0,24},{8,16},{16,8},{24,0},{1,25},{9,17},{17,9},{25,1},{2,26},{10... | collective-permute-start | bytes 393224 | tf_op jit(solution)/shard_map/ppermute | solution.py:180
  30.9 0.0 collective-permute-start.14
  30.9 2.1 %collective-permute-done.7.refs_1_ = f32[128,256]{1,0:T(8,128)S(1)} collective-permute-done((f32[128,256]{1,0:T(8,128)S(1)}, f32[128,256]{1,0:T(8,128)S(1)}, u32[]{:S(2)}, u32[]{:S(2)}) %collective-permute-start.7) | collective-permute-done | bytes 131104 | tf_op jit(solution)/shard_map/ppermute | solution.py:180
  33.0 3.2 %collective-permute-done.8.refs_2_ = f32[128,256]{1,0:T(8,128)S(1)} collective-permute-done((f32[128,256]{1,0:T(8,128)S(1)}, f32[128,256]{1,0:T(8,128)S(1)}, u32[]{:S(2)}, u32[]{:S(2)}) %collective-permute-start.8) | collective-permute-done | bytes 131104 | tf_op jit(solution)/shard_map/ppermute | solution.py:180
  36.2 0.0 collective-permute-done.9.refs_3_
  36.2 0.4 shard_map.126
  36.6 0.1 collective-permute-start.10
  36.7 2.4 %collective-permute-start.11 = (f32[64,256]{1,0:T(8,128)S(1)}, f32[64,256]{1,0:T(8,128)S(1)}, u32[]{:S(2)}, u32[]{:S(2)}) collective-permute-start(f32[64,256]{1,0:T(8,128)S(1)} %get-tuple-element.50), channel_id=1, source_target_pairs={{0,4},{1,5},{2,6},{3,7},{4,0},{5,1},{6,2},{7,3},{8,12},{9,13},{10,... | collective-permute-start | bytes 196616 | tf_op jit(solution)/shard_map/ppermute | solution.py:180
  39.1 2.0 %collective-permute-start.12 = (f32[64,256]{1,0:T(8,128)S(1)}, f32[64,256]{1,0:T(8,128)S(1)}, u32[]{:S(2)}, u32[]{:S(2)}) collective-permute-start(f32[64,256]{1,0:T(8,128)S(1)} %get-tuple-element.51), channel_id=1, source_target_pairs={{0,6},{1,7},{2,4},{3,5},{4,2},{5,3},{6,0},{7,1},{8,14},{9,15},{10,... | collective-permute-start | bytes 196616 | tf_op jit(solution)/shard_map/ppermute | solution.py:180
  41.1 0.0 collective-permute-done.14
  41.1 0.1 collective-permute-start.15
  41.2 2.4 %collective-permute-start.16 = (f32[40,256]{1,0:T(8,128)S(1)}, f32[40,256]{1,0:T(8,128)S(1)}, u32[]{:S(2)}, u32[]{:S(2)}) collective-permute-start(f32[40,256]{1,0:T(8,128)S(1)} %get-tuple-element.57), channel_id=1, source_target_pairs={{0,4},{1,5},{2,6},{3,7},{4,0},{5,1},{6,2},{7,3},{8,12},{9,13},{10,... | collective-permute-start | bytes 122888 | tf_op jit(solution)/shard_map/ppermute | solution.py:180
  43.6 0.0 collective-permute-done.10
  43.6 2.0 %collective-permute-start.17 = (f32[40,256]{1,0:T(8,128)S(1)}, f32[40,256]{1,0:T(8,128)S(1)}, u32[]{:S(2)}, u32[]{:S(2)}) collective-permute-start(f32[40,256]{1,0:T(8,128)S(1)} %get-tuple-element.56), channel_id=1, source_target_pairs={{0,6},{1,7},{2,4},{3,5},{4,2},{5,3},{6,0},{7,1},{8,14},{9,15},{10,... | collective-permute-start | bytes 122888 | tf_op jit(solution)/shard_map/ppermute | solution.py:180
  45.6 0.0 collective-permute-done.11
  45.6 0.4 collective-permute-done.15
  46.0 0.7 collective-permute-done.16
  46.7 2.7 %collective-permute-done.17 = f32[40,256]{1,0:T(8,128)S(1)} collective-permute-done((f32[40,256]{1,0:T(8,128)S(1)}, f32[40,256]{1,0:T(8,128)S(1)}, u32[]{:S(2)}, u32[]{:S(2)}) %collective-permute-start.17) | collective-permute-done | bytes 40992 | tf_op jit(solution)/shard_map/ppermute | solution.py:180
  49.4 1.1 %collective-permute-start.18 = (f32[40,256]{1,0:T(8,128)S(1)}, f32[40,256]{1,0:T(8,128)S(1)}, u32[]{:S(2)}, u32[]{:S(2)}) collective-permute-start(f32[40,256]{1,0:T(8,128)S(1)} %fusion), channel_id=1, source_target_pairs={{0,8},{8,0},{16,24},{24,16},{1,9},{9,1},{17,25},{25,17},{2,10},{10... | collective-permute-start | bytes 122888 | tf_op jit(solution)/shard_map/ppermute | solution.py:180
  50.5 1.2 %collective-permute-start.19 = (f32[40,256]{1,0:T(8,128)S(1)}, f32[40,256]{1,0:T(8,128)S(1)}, u32[]{:S(2)}, u32[]{:S(2)}) collective-permute-start(f32[40,256]{1,0:T(8,128)S(1)} %fusion), channel_id=1, source_target_pairs={{0,16},{8,24},{16,0},{24,8},{1,17},{9,25},{17,1},{25,9},{2,18},{10... | collective-permute-start | bytes 122888 | tf_op jit(solution)/shard_map/ppermute | solution.py:180
  51.6 1.3 %collective-permute-start.20 = (f32[40,256]{1,0:T(8,128)S(1)}, f32[40,256]{1,0:T(8,128)S(1)}, u32[]{:S(2)}, u32[]{:S(2)}) collective-permute-start(f32[40,256]{1,0:T(8,128)S(1)} %fusion), channel_id=1, source_target_pairs={{0,24},{8,16},{16,8},{24,0},{1,25},{9,17},{17,9},{25,1},{2,26},{10... | collective-permute-start | bytes 122888 | tf_op jit(solution)/shard_map/ppermute | solution.py:180
  53.0 0.0 collective-permute-done.12
  53.0 0.5 collective-permute-done.18
  53.5 1.0 %collective-permute-done.19 = f32[40,256]{1,0:T(8,128)S(1)} collective-permute-done((f32[40,256]{1,0:T(8,128)S(1)}, f32[40,256]{1,0:T(8,128)S(1)}, u32[]{:S(2)}, u32[]{:S(2)}) %collective-permute-start.19) | collective-permute-done | bytes 40992 | tf_op jit(solution)/shard_map/ppermute | solution.py:180
  54.5 2.1 %collective-permute-done.20 = f32[40,256]{1,0:T(8,128)S(1)} collective-permute-done((f32[40,256]{1,0:T(8,128)S(1)}, f32[40,256]{1,0:T(8,128)S(1)}, u32[]{:S(2)}, u32[]{:S(2)}) %collective-permute-start.20) | collective-permute-done | bytes 40992 | tf_op jit(solution)/shard_map/ppermute | solution.py:180
  56.6 0.1 collective-permute-start.21
  56.6 2.6 %collective-permute-start.22 = (f32[32,256]{1,0:T(8,128)S(1)}, f32[32,256]{1,0:T(8,128)S(1)}, u32[]{:S(2)}, u32[]{:S(2)}) collective-permute-start(f32[32,256]{1,0:T(8,128)S(1)} %slice.100), channel_id=1, source_target_pairs={{0,4},{1,5},{2,6},{3,7},{4,0},{5,1},{6,2},{7,3},{8,12},{9,13},{10,... | collective-permute-start | bytes 98312 | tf_op jit(solution)/shard_map/ppermute | solution.py:180
  59.2 1.8 %collective-permute-start.23 = (f32[32,256]{1,0:T(8,128)S(1)}, f32[32,256]{1,0:T(8,128)S(1)}, u32[]{:S(2)}, u32[]{:S(2)}) collective-permute-start(f32[32,256]{1,0:T(8,128)S(1)} %slice.100), channel_id=1, source_target_pairs={{0,6},{1,7},{2,4},{3,5},{4,2},{5,3},{6,0},{7,1},{8,14},{9,15},{10,... | collective-permute-start | bytes 98312 | tf_op jit(solution)/shard_map/ppermute | solution.py:180
  61.0 0.1 collective-permute-start.13
  61.1 0.0 collective-permute-done.21
  61.1 0.4 collective-permute-done.22
  61.5 3.4 %collective-permute-done.23 = f32[32,256]{1,0:T(8,128)S(1)} collective-permute-done((f32[32,256]{1,0:T(8,128)S(1)}, f32[32,256]{1,0:T(8,128)S(1)}, u32[]{:S(2)}, u32[]{:S(2)}) %collective-permute-start.23) | collective-permute-done | bytes 32800 | tf_op jit(solution)/shard_map/ppermute | solution.py:180
  64.9 0.1 collective-permute-start.24
  65.0 0.7 %shard_map.125 = f32[128,256]{1,0:T(8,128)} custom-call(f32[128,256]{1,0:T(8,128)S(1)} %get-tuple-element.43.pre_ref), custom_call_target="tpu_custom_call" | custom-call | bytes 262144 | tf_op jit(solution)/shard_map/pallas_call | solution.py:39
  65.7 0.0 collective-permute-done.13.partner_ref
  65.7 1.1 %shard_map.127 = f32[128,256]{1,0:T(8,128)} custom-call(s32[1,256]{1,0:T(1,128)S(1)} %get-tuple-element.44.wanted_ref, bf16[256,256]{1,0:T(8,128)(2,1)S(1)} %get-tuple-element.40.refs_4_.high_ref, bf16[256,256]{1,0:T(8,128)(2,1)S(1)} %get-tuple-element.41.refs_5_.low_ref, f32[128,256]{1,0:T(8,128)S(1)} %pad_maximum_fusion.2.own_ref, ...), custom_call_target="tpu_custom_call" | custom-call | flops 50331648 | bytes 656384 | tf_op jit(solution)/shard_map/pallas_call | solution.py:39
  66.8 0.0 collective-permute-done.24.partner_ref
  66.8 0.7 %shard_map.128 = (f32[256,256]{1,0:T(8,128)}, f32[1,256]{1,0:T(1,128)}) custom-call(f32[40,256]{1,0:T(8,128)S(1)} %add_add_fusion.summed_ref, f32[128,256]{1,0:T(8,128)S(1)} %pad_maximum_fusion.4.own_ref, f32[128,256]{1,0:T(8,128)S(1)} %collective-permute-done.24.partner_ref), custom_call_target="tpu_custom_call" | custom-call | bytes 566272 | tf_op jit(solution)/shard_map/pallas_call | solution.py:39
  (19 shorter events, 0.2 us)
Async XLA Ops:
  1.8 5.7 %collective-permute-start = (f32[64,256]{1,0:T(8,128)S(1)}, f32[64,256]{1,0:T(8,128)S(1)}, u32[]{:S(2)}, u32[]{:S(2)}) collective-permute-start(f32[64,256]{1,0:T(8,128)S(1)} %get-tuple-element.33), channel_id=1, source_target_pairs={{0,2},{1,3},{2,0},{3,1},{4,6},{5,7},{6,4},{7,5},{8,10},{9,11},{10,... | collective-permute-start | bytes 196616 | tf_op jit(solution)/shard_map/ppermute | solution.py:180
  4.9 7.3 %collective-permute-start.1 = (f32[64,256]{1,0:T(8,128)S(1)}, f32[64,256]{1,0:T(8,128)S(1)}, u32[]{:S(2)}, u32[]{:S(2)}) collective-permute-start(f32[64,256]{1,0:T(8,128)S(1)} %get-tuple-element.34), channel_id=1, source_target_pairs={{0,4},{1,5},{2,6},{3,7},{4,0},{5,1},{6,2},{7,3},{8,12},{9,13},{10,... | collective-permute-start | bytes 196616 | tf_op jit(solution)/shard_map/ppermute | solution.py:180
  7.5 6.1 %collective-permute-start.2 = (f32[64,256]{1,0:T(8,128)S(1)}, f32[64,256]{1,0:T(8,128)S(1)}, u32[]{:S(2)}, u32[]{:S(2)}) collective-permute-start(f32[64,256]{1,0:T(8,128)S(1)} %get-tuple-element.35), channel_id=1, source_target_pairs={{0,6},{1,7},{2,4},{3,5},{4,2},{5,3},{6,0},{7,1},{8,14},{9,15},{10,... | collective-permute-start | bytes 196616 | tf_op jit(solution)/shard_map/ppermute | solution.py:180
  13.6 2.8 %collective-permute-start.3 = (f32[128,256]{1,0:T(8,128)S(1)}, f32[128,256]{1,0:T(8,128)S(1)}, u32[]{:S(2)}, u32[]{:S(2)}) collective-permute-start(f32[128,256]{1,0:T(8,128)S(1)} %pad_maximum_fusion.1), channel_id=1, source_target_pairs={{0,1},{1,0},{2,3},{3,2},{4,5},{5,4},{6,7},{7,6},{8,9},{9,8},{10,11... | collective-permute-start | bytes 393224 | tf_op jit(solution)/shard_map/ppermute | solution.py:180
  16.4 4.0 %copy-start = (f32[256,256]{1,0:T(8,128)S(1)}, f32[256,256]{1,0:T(8,128)}, u32[]{:S(2)}) copy-start(f32[256,256]{1,0:T(8,128)} %weight_ref.1) | copy-start | bytes 786436
  16.8 6.4 %collective-permute-start.4 = (f32[128,256]{1,0:T(8,128)S(1)}, f32[128,256]{1,0:T(8,128)S(1)}, u32[]{:S(2)}, u32[]{:S(2)}) collective-permute-start(f32[128,256]{1,0:T(8,128)S(1)} %get-tuple-element.37), channel_id=1, source_target_pairs={{0,8},{8,0},{16,24},{24,16},{1,9},{9,1},{17,25},{25,17},{2,10},{10... | collective-permute-start | bytes 393224 | tf_op jit(solution)/shard_map/ppermute | solution.py:180
  18.3 8.4 %collective-permute-start.5 = (f32[128,256]{1,0:T(8,128)S(1)}, f32[128,256]{1,0:T(8,128)S(1)}, u32[]{:S(2)}, u32[]{:S(2)}) collective-permute-start(f32[128,256]{1,0:T(8,128)S(1)} %get-tuple-element.38), channel_id=1, source_target_pairs={{0,16},{8,24},{16,0},{24,8},{1,17},{9,25},{17,1},{25,9},{2,18},{10... | collective-permute-start | bytes 393224 | tf_op jit(solution)/shard_map/ppermute | solution.py:180
  19.8 0.7 %copy-start.2 = (f32[256]{0:T(256)S(1)}, f32[256]{0:T(256)}, u32[]{:S(2)}) copy-start(f32[256]{0:T(256)} %param.11) | copy-start | bytes 3076
  19.9 6.9 %collective-permute-start.6 = (f32[128,256]{1,0:T(8,128)S(1)}, f32[128,256]{1,0:T(8,128)S(1)}, u32[]{:S(2)}, u32[]{:S(2)}) collective-permute-start(f32[128,256]{1,0:T(8,128)S(1)} %get-tuple-element.39), channel_id=1, source_target_pairs={{0,24},{8,16},{16,8},{24,0},{1,25},{9,17},{17,9},{25,1},{2,26},{10... | collective-permute-start | bytes 393224 | tf_op jit(solution)/shard_map/ppermute | solution.py:180
  20.5 6.2 %copy-start.1 = (f32[128,256]{1,0:T(8,128)S(1)}, f32[128,256]{1,0:T(8,128)}, u32[]{:S(2)}) copy-start(f32[128,256]{1,0:T(8,128)} %refs_7_.1) | copy-start | bytes 393220
  27.4 5.6 %collective-permute-start.7 = (f32[128,256]{1,0:T(8,128)S(1)}, f32[128,256]{1,0:T(8,128)S(1)}, u32[]{:S(2)}, u32[]{:S(2)}) collective-permute-start(f32[128,256]{1,0:T(8,128)S(1)} %get-tuple-element.47.refs_0_), channel_id=1, source_target_pairs={{0,8},{8,0},{16,24},{24,16},{1,9},{9,1},{17,25},{25,17},{2,10},{10... | collective-permute-start | bytes 393224 | tf_op jit(solution)/shard_map/ppermute | solution.py:180
  28.7 7.6 %collective-permute-start.8 = (f32[128,256]{1,0:T(8,128)S(1)}, f32[128,256]{1,0:T(8,128)S(1)}, u32[]{:S(2)}, u32[]{:S(2)}) collective-permute-start(f32[128,256]{1,0:T(8,128)S(1)} %get-tuple-element.47.refs_0_), channel_id=1, source_target_pairs={{0,16},{8,24},{16,0},{24,8},{1,17},{9,25},{17,1},{25,9},{2,18},{10... | collective-permute-start | bytes 393224 | tf_op jit(solution)/shard_map/ppermute | solution.py:180
  29.5 6.8 %collective-permute-start.9 = (f32[128,256]{1,0:T(8,128)S(1)}, f32[128,256]{1,0:T(8,128)S(1)}, u32[]{:S(2)}, u32[]{:S(2)}) collective-permute-start(f32[128,256]{1,0:T(8,128)S(1)} %get-tuple-element.47.refs_0_), channel_id=1, source_target_pairs={{0,24},{8,16},{16,8},{24,0},{1,25},{9,17},{17,9},{25,1},{2,26},{10... | collective-permute-start | bytes 393224 | tf_op jit(solution)/shard_map/ppermute | solution.py:180
  30.9 10.2 %collective-permute-start.14 = (f32[160,256]{1,0:T(8,128)S(1)}, f32[160,256]{1,0:T(8,128)S(1)}, u32[]{:S(2)}, u32[]{:S(2)}) collective-permute-start(f32[160,256]{1,0:T(8,128)S(1)} %get-tuple-element.53), channel_id=1, source_target_pairs={{0,1},{1,0},{2,3},{3,2},{4,5},{5,4},{6,7},{7,6},{8,9},{9,8},{10,11... | collective-permute-start | bytes 491528 | tf_op jit(solution)/shard_map/ppermute | solution.py:180
  36.6 7.0 %collective-permute-start.10 = (f32[64,256]{1,0:T(8,128)S(1)}, f32[64,256]{1,0:T(8,128)S(1)}, u32[]{:S(2)}, u32[]{:S(2)}) collective-permute-start(f32[64,256]{1,0:T(8,128)S(1)} %get-tuple-element.49), channel_id=1, source_target_pairs={{0,2},{1,3},{2,0},{3,1},{4,6},{5,7},{6,4},{7,5},{8,10},{9,11},{10,... | collective-permute-start | bytes 196616 | tf_op jit(solution)/shard_map/ppermute | solution.py:180
  36.7 8.9 %collective-permute-start.11 = (f32[64,256]{1,0:T(8,128)S(1)}, f32[64,256]{1,0:T(8,128)S(1)}, u32[]{:S(2)}, u32[]{:S(2)}) collective-permute-start(f32[64,256]{1,0:T(8,128)S(1)} %get-tuple-element.50), channel_id=1, source_target_pairs={{0,4},{1,5},{2,6},{3,7},{4,0},{5,1},{6,2},{7,3},{8,12},{9,13},{10,... | collective-permute-start | bytes 196616 | tf_op jit(solution)/shard_map/ppermute | solution.py:180
  39.1 13.9 %collective-permute-start.12 = (f32[64,256]{1,0:T(8,128)S(1)}, f32[64,256]{1,0:T(8,128)S(1)}, u32[]{:S(2)}, u32[]{:S(2)}) collective-permute-start(f32[64,256]{1,0:T(8,128)S(1)} %get-tuple-element.51), channel_id=1, source_target_pairs={{0,6},{1,7},{2,4},{3,5},{4,2},{5,3},{6,0},{7,1},{8,14},{9,15},{10,... | collective-permute-start | bytes 196616 | tf_op jit(solution)/shard_map/ppermute | solution.py:180
  41.1 4.9 %collective-permute-start.15 = (f32[40,256]{1,0:T(8,128)S(1)}, f32[40,256]{1,0:T(8,128)S(1)}, u32[]{:S(2)}, u32[]{:S(2)}) collective-permute-start(f32[40,256]{1,0:T(8,128)S(1)} %get-tuple-element.58), channel_id=1, source_target_pairs={{0,2},{1,3},{2,0},{3,1},{4,6},{5,7},{6,4},{7,5},{8,10},{9,11},{10,... | collective-permute-start | bytes 122888 | tf_op jit(solution)/shard_map/ppermute | solution.py:180
  41.2 5.4 %collective-permute-start.16 = (f32[40,256]{1,0:T(8,128)S(1)}, f32[40,256]{1,0:T(8,128)S(1)}, u32[]{:S(2)}, u32[]{:S(2)}) collective-permute-start(f32[40,256]{1,0:T(8,128)S(1)} %get-tuple-element.57), channel_id=1, source_target_pairs={{0,4},{1,5},{2,6},{3,7},{4,0},{5,1},{6,2},{7,3},{8,12},{9,13},{10,... | collective-permute-start | bytes 122888 | tf_op jit(solution)/shard_map/ppermute | solution.py:180
  43.6 5.8 %collective-permute-start.17 = (f32[40,256]{1,0:T(8,128)S(1)}, f32[40,256]{1,0:T(8,128)S(1)}, u32[]{:S(2)}, u32[]{:S(2)}) collective-permute-start(f32[40,256]{1,0:T(8,128)S(1)} %get-tuple-element.56), channel_id=1, source_target_pairs={{0,6},{1,7},{2,4},{3,5},{4,2},{5,3},{6,0},{7,1},{8,14},{9,15},{10,... | collective-permute-start | bytes 122888 | tf_op jit(solution)/shard_map/ppermute | solution.py:180
  49.4 4.1 %collective-permute-start.18 = (f32[40,256]{1,0:T(8,128)S(1)}, f32[40,256]{1,0:T(8,128)S(1)}, u32[]{:S(2)}, u32[]{:S(2)}) collective-permute-start(f32[40,256]{1,0:T(8,128)S(1)} %fusion), channel_id=1, source_target_pairs={{0,8},{8,0},{16,24},{24,16},{1,9},{9,1},{17,25},{25,17},{2,10},{10... | collective-permute-start | bytes 122888 | tf_op jit(solution)/shard_map/ppermute | solution.py:180
  50.5 4.0 %collective-permute-start.19 = (f32[40,256]{1,0:T(8,128)S(1)}, f32[40,256]{1,0:T(8,128)S(1)}, u32[]{:S(2)}, u32[]{:S(2)}) collective-permute-start(f32[40,256]{1,0:T(8,128)S(1)} %fusion), channel_id=1, source_target_pairs={{0,16},{8,24},{16,0},{24,8},{1,17},{9,25},{17,1},{25,9},{2,18},{10... | collective-permute-start | bytes 122888 | tf_op jit(solution)/shard_map/ppermute | solution.py:180
  51.6 4.9 %collective-permute-start.20 = (f32[40,256]{1,0:T(8,128)S(1)}, f32[40,256]{1,0:T(8,128)S(1)}, u32[]{:S(2)}, u32[]{:S(2)}) collective-permute-start(f32[40,256]{1,0:T(8,128)S(1)} %fusion), channel_id=1, source_target_pairs={{0,24},{8,16},{16,8},{24,0},{1,25},{9,17},{17,9},{25,1},{2,26},{10... | collective-permute-start | bytes 122888 | tf_op jit(solution)/shard_map/ppermute | solution.py:180
  56.6 4.5 %collective-permute-start.21 = (f32[32,256]{1,0:T(8,128)S(1)}, f32[32,256]{1,0:T(8,128)S(1)}, u32[]{:S(2)}, u32[]{:S(2)}) collective-permute-start(f32[32,256]{1,0:T(8,128)S(1)} %slice.100), channel_id=1, source_target_pairs={{0,2},{1,3},{2,0},{3,1},{4,6},{5,7},{6,4},{7,5},{8,10},{9,11},{10,... | collective-permute-start | bytes 98312 | tf_op jit(solution)/shard_map/ppermute | solution.py:180
  56.6 4.9 %collective-permute-start.22 = (f32[32,256]{1,0:T(8,128)S(1)}, f32[32,256]{1,0:T(8,128)S(1)}, u32[]{:S(2)}, u32[]{:S(2)}) collective-permute-start(f32[32,256]{1,0:T(8,128)S(1)} %slice.100), channel_id=1, source_target_pairs={{0,4},{1,5},{2,6},{3,7},{4,0},{5,1},{6,2},{7,3},{8,12},{9,13},{10,... | collective-permute-start | bytes 98312 | tf_op jit(solution)/shard_map/ppermute | solution.py:180
  59.2 5.7 %collective-permute-start.23 = (f32[32,256]{1,0:T(8,128)S(1)}, f32[32,256]{1,0:T(8,128)S(1)}, u32[]{:S(2)}, u32[]{:S(2)}) collective-permute-start(f32[32,256]{1,0:T(8,128)S(1)} %slice.100), channel_id=1, source_target_pairs={{0,6},{1,7},{2,4},{3,5},{4,2},{5,3},{6,0},{7,1},{8,14},{9,15},{10,... | collective-permute-start | bytes 98312 | tf_op jit(solution)/shard_map/ppermute | solution.py:180
  61.0 4.7 %collective-permute-start.13 = (f32[128,256]{1,0:T(8,128)S(1)}, f32[128,256]{1,0:T(8,128)S(1)}, u32[]{:S(2)}, u32[]{:S(2)}) collective-permute-start(f32[128,256]{1,0:T(8,128)S(1)} %pad_maximum_fusion.3), channel_id=1, source_target_pairs={{0,1},{1,0},{2,3},{3,2},{4,5},{5,4},{6,7},{7,6},{8,9},{9,8},{10,11... | collective-permute-start | bytes 393224 | tf_op jit(solution)/shard_map/ppermute | solution.py:180
  64.9 1.9 %collective-permute-start.24 = (f32[128,256]{1,0:T(8,128)S(1)}, f32[128,256]{1,0:T(8,128)S(1)}, u32[]{:S(2)}, u32[]{:S(2)}) collective-permute-start(f32[128,256]{1,0:T(8,128)S(1)} %pad_maximum_fusion.4.own_ref), channel_id=1, source_target_pairs={{0,1},{1,0},{2,3},{3,2},{4,5},{5,4},{6,7},{7,6},{8,9},{9,8},{10,11... | collective-permute-start | bytes 393224 | tf_op jit(solution)/shard_map/ppermute | solution.py:180
where the time goes:
time: 67.8 us; the launch traced here: 67.6 us
  starting transfers between devices  29.9 us (44%)
  waiting for transfers between devices  28.5 us (42%)
  Pallas kernels  7.26 us (11%)
  between operations  1.51 us (2%)
    ppermute x25, starting transfers between devices, exchange(): return lax.ppermute(value, axis, [(i, i ^ shift) for i in range(size)])  29.9 us
    ppermute x25, waiting for transfers between devices, exchange(): return lax.ppermute(value, axis, [(i, i ^ shift) for i in range(size)])  28.5 us
    pallas_call x9, Pallas kernels, call(): pl.pallas_call(kernel, out_shape=outs, in_specs=[pl.BlockSpec(memory_spac...  7.26 us
  transfers between devices with their start and end apart: 25, of which 14 were waited for; matrix products, arithmetic and copies ran while one was open for 0% of the time, Pallas kernels for 6%

commit v1 on v0

--- a/solution.py
+++ b/solution.py
@@ -11,6 +11,7 @@
 BS = 64
 LANES = 128
 PAD = 8
+PARTS = 4
 FLOOR = 16 * 2**20
 F32 = jnp.float32
 BF16 = jnp.bfloat16
@@ -84,19 +85,29 @@
         buffer[rows_at(lax.bitwise_xor(me, 2 * pair + 1), per), :] = partner_ref[rows, :]
 
 
+def copies_of(source, target, sems, first):
+    rows = source.shape[0] // PARTS
+    copies = []
+    for k in range(PARTS):
+        part = slice(k * rows, (k + 1) * rows)
+        copies.append(
+            pltpu.make_async_copy(source.at[part, :], target.at[part, :], sems.at[first + k])
+        )
+    return copies
+
+
 def gather_rows(list_hbm, feat_hbm, *refs):
     outs, wanted_ref, feat_ref, buffer, sems = refs[:-4], refs[-4], refs[-3], refs[-2], refs[-1]
     me = lax.axis_index("row")
     slots = buffer.shape[0]
-    copies = [
-        pltpu.make_async_copy(feat_hbm, feat_ref, sems.at[0]),
-        pltpu.make_async_copy(list_hbm.at[:, rows_at(me, slots)], wanted_ref, sems.at[1]),
-    ]
+    wanted = pltpu.make_async_copy(list_hbm.at[:, rows_at(me, slots)], wanted_ref, sems.at[PARTS])
+    copies = copies_of(feat_hbm, feat_ref, sems, 0)
+    for copy in [wanted, *copies]:
+        copy.start()
+    wanted.wait()
+    pick = one_hot(wanted_ref[...], feat_ref.shape[0]).T
     for copy in copies:
-        copy.start()
-    copies[1].wait()
-    pick = one_hot(wanted_ref[...], feat_ref.shape[0]).T
-    copies[0].wait()
+        copy.wait()
     high, low = split(feat_ref[...])
     buffer[...] = mm(pick, high, NN) + mm(pick, low, NN)
     put_pairs(outs, buffer, me, outs[0].shape[0] // 2)
@@ -209,7 +220,7 @@
         gather_rows,
         [shape(2 * per)] * pairs + [jax.ShapeDtypeStruct((1, slots), jnp.int32)],
         [pltpu.with_memory_space_constraint(x, pltpu.HBM) for x in (send_list, node_feat)],
-        [vmem(nodes), vmem(slots), pltpu.SemaphoreType.DMA((2,))],
+        [vmem(nodes), vmem(slots), pltpu.SemaphoreType.DMA((PARTS + 1,))],
         hbm=(0, 1),
     )
     border = swap_rows(sends)
@@ -231,7 +242,7 @@
             pltpu.VMEM((1, capacity), jnp.int32),
             pltpu.VMEM((capacity, BS * BS), F32),
             pltpu.VMEM((slots // LANES, rows, LANES), F32),
-            pltpu.SemaphoreType.DMA((3,)),
+            pltpu.SemaphoreType.DMA((PARTS + 2,)),
         ],
         flops=4 * row_blocks * col_blocks * capacity * BS * BS,
         hbm=(1, 2, 3),
@@ -292,14 +303,14 @@
 
 def build(shard_blocks, live_ref, rows_hbm, cols_hbm, blocks_hbm, high_ref, low_ref, *refs):
     rows_ref, cols_ref, blocks_ref, dense, sems = refs
-    copies = [
-        pltpu.make_async_copy(blocks_hbm, blocks_ref, sems.at[0]),
-        pltpu.make_async_copy(rows_hbm, rows_ref, sems.at[1]),
-        pltpu.make_async_copy(cols_hbm, cols_ref, sems.at[2]),
+    places = [
+        pltpu.make_async_copy(rows_hbm, rows_ref, sems.at[PARTS]),
+        pltpu.make_async_copy(cols_hbm, cols_ref, sems.at[PARTS + 1]),
     ]
-    for copy in copies:
+    copies = copies_of(blocks_hbm, blocks_ref, sems, 0)
+    for copy in [*places, *copies]:
         copy.start()
-    for copy in copies[1:]:
+    for copy in places:
         copy.wait()
     row_blocks = high_ref.shape[0] // BS
     col_blocks = high_ref.shape[1] // BS
@@ -311,7 +322,8 @@
     pair = lax.broadcasted_iota(jnp.int32, (pairs, capacity), 0)
     slot = lax.broadcasted_iota(jnp.int32, (pairs, capacity), 1)
     pick = ((pair == cols * row_blocks + rows) & (slot < live_ref[...])).astype(BF16)
-    copies[0].wait()
+    for copy in copies:
+        copy.wait()
     high, low = split(blocks_ref[...])
     product = mm(pick, high, NN) + mm(pick, low, NN)
     left = lax.broadcasted_iota(jnp.int32, (row_blocks, LANES), 1) < BS

time: 67.8 us -> 67.8 us (level)
  transfers between devices with their start and end apart: 25 -> 25, of which waited for: 14 -> 14; matrix products, arithmetic and copies ran while one was open for 0% -> 0% of each run, Pallas kernels for 6% -> 7%
where the time goes in v1:
time: 67.8 us; the launch traced here: 67.5 us
  starting transfers between devices  29.9 us (44%)
  waiting for transfers between devices  28.5 us (42%)
  Pallas kernels  7.23 us (11%)
  between operations  1.51 us (2%)
    ppermute x25, starting transfers between devices, exchange(): return lax.ppermute(value, axis, [(i, i ^ shift) for i in range(size)])  29.9 us
    ppermute x25, waiting for transfers between devices, exchange(): return lax.ppermute(value, axis, [(i, i ^ shift) for i in range(size)])  28.5 us
    pallas_call x9, Pallas kernels, call(): pl.pallas_call(kernel, out_shape=outs, in_specs=[pl.BlockSpec(memory_spac...  7.23 us
  transfers between devices with their start and end apart: 25, of which 14 were waited for; matrix products, arithmetic and copies ran while one was open for 0% of the time, Pallas kernels for 7%

profile of v1, /device:TPU:0, one launch (start us, length us, event | category | flops | bytes accessed | tf_op | source)
XLA Modules:
  0.0 67.5 jit_solution(12353245331749524755)
XLA Ops:
  0.6 1.1 %shard_map.121 = (f32[64,256]{1,0:T(8,128)S(1)}, f32[64,256]{1,0:T(8,128)S(1)}, f32[64,256]{1,0:T(8,128)S(1)}, f32[64,256]{1,0:T(8,128)S(1)}, s32[1,256]{1,0:T(1,128)S(1)}) custom-call(s32[1,2048]{1,0:T(1,128)} %list_hbm.1, f32[128,256]{1,0:T(8,128)} %feat_hbm.1), custom_call_target="tpu_custom_call" | custom-call | bytes 402432 | tf_op jit(solution)/shard_map/pallas_call | solution.py:40
  1.7 3.1 %collective-permute-start = (f32[64,256]{1,0:T(8,128)S(1)}, f32[64,256]{1,0:T(8,128)S(1)}, u32[]{:S(2)}, u32[]{:S(2)}) collective-permute-start(f32[64,256]{1,0:T(8,128)S(1)} %get-tuple-element.33), channel_id=1, source_target_pairs={{0,2},{1,3},{2,0},{3,1},{4,6},{5,7},{6,4},{7,5},{8,10},{9,11},{10,... | collective-permute-start | bytes 196616 | tf_op jit(solution)/shard_map/ppermute | solution.py:191
  4.9 2.6 %collective-permute-start.1 = (f32[64,256]{1,0:T(8,128)S(1)}, f32[64,256]{1,0:T(8,128)S(1)}, u32[]{:S(2)}, u32[]{:S(2)}) collective-permute-start(f32[64,256]{1,0:T(8,128)S(1)} %get-tuple-element.34), channel_id=1, source_target_pairs={{0,4},{1,5},{2,6},{3,7},{4,0},{5,1},{6,2},{7,3},{8,12},{9,13},{10,... | collective-permute-start | bytes 196616 | tf_op jit(solution)/shard_map/ppermute | solution.py:191
  7.5 0.0 collective-permute-start.2
  7.5 0.0 collective-permute-done
  7.5 4.6 %collective-permute-done.1 = f32[64,256]{1,0:T(8,128)S(1)} collective-permute-done((f32[64,256]{1,0:T(8,128)S(1)}, f32[64,256]{1,0:T(8,128)S(1)}, u32[]{:S(2)}, u32[]{:S(2)}) %collective-permute-start.1) | collective-permute-done | bytes 65568 | tf_op jit(solution)/shard_map/ppermute | solution.py:191
  12.1 1.4 %collective-permute-done.2 = f32[64,256]{1,0:T(8,128)S(1)} collective-permute-done((f32[64,256]{1,0:T(8,128)S(1)}, f32[64,256]{1,0:T(8,128)S(1)}, u32[]{:S(2)}, u32[]{:S(2)}) %collective-permute-start.2) | collective-permute-done | bytes 65568 | tf_op jit(solution)/shard_map/ppermute | solution.py:191
  13.6 0.1 collective-permute-start.3
  14.3 2.0 %shard_map.120 = (bf16[512,256]{1,0:T(8,128)(2,1)S(1)}, bf16[512,256]{1,0:T(8,128)(2,1)S(1)}) custom-call(s32[1,1]{1,0:T(1,128)S(6)} %copy.13.live_ref, s32[1,64]{1,0:T(1,128)} %bitcast.7, s32[1,64]{1,0:T(1,128)} %bitcast.8, f32[64,4096]{1,0:T(8,128)} %bitcast.6), custom_call_target="tpu_custom_call" | custom-call | flops 33554432 | bytes 1573380 | tf_op jit(solution)/shard_map/pallas_call | solution.py:40
  16.3 0.0 collective-permute-done.3.partner_ref
  16.3 0.0 copy-start
  16.3 0.4 shard_map.122
  16.7 1.6 %collective-permute-start.4 = (f32[128,256]{1,0:T(8,128)S(1)}, f32[128,256]{1,0:T(8,128)S(1)}, u32[]{:S(2)}, u32[]{:S(2)}) collective-permute-start(f32[128,256]{1,0:T(8,128)S(1)} %get-tuple-element.37), channel_id=1, source_target_pairs={{0,8},{8,0},{16,24},{24,16},{1,9},{9,1},{17,25},{25,17},{2,10},{10... | collective-permute-start | bytes 393224 | tf_op jit(solution)/shard_map/ppermute | solution.py:191
  18.3 1.5 %collective-permute-start.5 = (f32[128,256]{1,0:T(8,128)S(1)}, f32[128,256]{1,0:T(8,128)S(1)}, u32[]{:S(2)}, u32[]{:S(2)}) collective-permute-start(f32[128,256]{1,0:T(8,128)S(1)} %get-tuple-element.38), channel_id=1, source_target_pairs={{0,16},{8,24},{16,0},{24,8},{1,17},{9,25},{17,1},{25,9},{2,18},{10... | collective-permute-start | bytes 393224 | tf_op jit(solution)/shard_map/ppermute | solution.py:191
  19.8 0.0 copy-start.2
  19.8 0.5 collective-permute-start.6
  20.3 0.0 copy-done
  20.3 0.2 copy-done.2
  20.5 0.2 shard_map.123
  20.7 2.4 %collective-permute-done.4.refs_1_ = f32[128,256]{1,0:T(8,128)S(1)} collective-permute-done((f32[128,256]{1,0:T(8,128)S(1)}, f32[128,256]{1,0:T(8,128)S(1)}, u32[]{:S(2)}, u32[]{:S(2)}) %collective-permute-start.4) | collective-permute-done | bytes 131104 | tf_op jit(solution)/shard_map/ppermute | solution.py:191
  23.1 3.6 %collective-permute-done.5.refs_2_ = f32[128,256]{1,0:T(8,128)S(1)} collective-permute-done((f32[128,256]{1,0:T(8,128)S(1)}, f32[128,256]{1,0:T(8,128)S(1)}, u32[]{:S(2)}, u32[]{:S(2)}) %collective-permute-start.5) | collective-permute-done | bytes 131104 | tf_op jit(solution)/shard_map/ppermute | solution.py:191
  26.7 0.0 collective-permute-done.6.refs_3_
  26.7 0.0 copy-done.1
  26.7 0.6 shard_map.124
  27.3 1.3 %collective-permute-start.7 = (f32[128,256]{1,0:T(8,128)S(1)}, f32[128,256]{1,0:T(8,128)S(1)}, u32[]{:S(2)}, u32[]{:S(2)}) collective-permute-start(f32[128,256]{1,0:T(8,128)S(1)} %get-tuple-element.47.refs_0_), channel_id=1, source_target_pairs={{0,8},{8,0},{16,24},{24,16},{1,9},{9,1},{17,25},{25,17},{2,10},{10... | collective-permute-start | bytes 393224 | tf_op jit(solution)/shard_map/ppermute | solution.py:191
  28.6 0.8 %collective-permute-start.8 = (f32[128,256]{1,0:T(8,128)S(1)}, f32[128,256]{1,0:T(8,128)S(1)}, u32[]{:S(2)}, u32[]{:S(2)}) collective-permute-start(f32[128,256]{1,0:T(8,128)S(1)} %get-tuple-element.47.refs_0_), channel_id=1, source_target_pairs={{0,16},{8,24},{16,0},{24,8},{1,17},{9,25},{17,1},{25,9},{2,18},{10... | collective-permute-start | bytes 393224 | tf_op jit(solution)/shard_map/ppermute | solution.py:191
  29.5 1.4 %collective-permute-start.9 = (f32[128,256]{1,0:T(8,128)S(1)}, f32[128,256]{1,0:T(8,128)S(1)}, u32[]{:S(2)}, u32[]{:S(2)}) collective-permute-start(f32[128,256]{1,0:T(8,128)S(1)} %get-tuple-element.47.refs_0_), channel_id=1, source_target_pairs={{0,24},{8,16},{16,8},{24,0},{1,25},{9,17},{17,9},{25,1},{2,26},{10... | collective-permute-start | bytes 393224 | tf_op jit(solution)/shard_map/ppermute | solution.py:191
  30.9 0.0 collective-permute-start.14
  30.9 2.1 %collective-permute-done.7.refs_1_ = f32[128,256]{1,0:T(8,128)S(1)} collective-permute-done((f32[128,256]{1,0:T(8,128)S(1)}, f32[128,256]{1,0:T(8,128)S(1)}, u32[]{:S(2)}, u32[]{:S(2)}) %collective-permute-start.7) | collective-permute-done | bytes 131104 | tf_op jit(solution)/shard_map/ppermute | solution.py:191
  33.0 3.2 %collective-permute-done.8.refs_2_ = f32[128,256]{1,0:T(8,128)S(1)} collective-permute-done((f32[128,256]{1,0:T(8,128)S(1)}, f32[128,256]{1,0:T(8,128)S(1)}, u32[]{:S(2)}, u32[]{:S(2)}) %collective-permute-start.8) | collective-permute-done | bytes 131104 | tf_op jit(solution)/shard_map/ppermute | solution.py:191
  36.2 0.0 collective-permute-done.9.refs_3_
  36.2 0.4 shard_map.126
  36.6 0.1 collective-permute-start.10
  36.7 2.4 %collective-permute-start.11 = (f32[64,256]{1,0:T(8,128)S(1)}, f32[64,256]{1,0:T(8,128)S(1)}, u32[]{:S(2)}, u32[]{:S(2)}) collective-permute-start(f32[64,256]{1,0:T(8,128)S(1)} %get-tuple-element.50), channel_id=1, source_target_pairs={{0,4},{1,5},{2,6},{3,7},{4,0},{5,1},{6,2},{7,3},{8,12},{9,13},{10,... | collective-permute-start | bytes 196616 | tf_op jit(solution)/shard_map/ppermute | solution.py:191
  39.0 2.0 %collective-permute-start.12 = (f32[64,256]{1,0:T(8,128)S(1)}, f32[64,256]{1,0:T(8,128)S(1)}, u32[]{:S(2)}, u32[]{:S(2)}) collective-permute-start(f32[64,256]{1,0:T(8,128)S(1)} %get-tuple-element.51), channel_id=1, source_target_pairs={{0,6},{1,7},{2,4},{3,5},{4,2},{5,3},{6,0},{7,1},{8,14},{9,15},{10,... | collective-permute-start | bytes 196616 | tf_op jit(solution)/shard_map/ppermute | solution.py:191
  41.1 0.0 collective-permute-done.14
  41.1 0.1 collective-permute-start.15
  41.2 2.4 %collective-permute-start.16 = (f32[40,256]{1,0:T(8,128)S(1)}, f32[40,256]{1,0:T(8,128)S(1)}, u32[]{:S(2)}, u32[]{:S(2)}) collective-permute-start(f32[40,256]{1,0:T(8,128)S(1)} %get-tuple-element.57), channel_id=1, source_target_pairs={{0,4},{1,5},{2,6},{3,7},{4,0},{5,1},{6,2},{7,3},{8,12},{9,13},{10,... | collective-permute-start | bytes 122888 | tf_op jit(solution)/shard_map/ppermute | solution.py:191
  43.6 0.0 collective-permute-done.10
  43.6 2.0 %collective-permute-start.17 = (f32[40,256]{1,0:T(8,128)S(1)}, f32[40,256]{1,0:T(8,128)S(1)}, u32[]{:S(2)}, u32[]{:S(2)}) collective-permute-start(f32[40,256]{1,0:T(8,128)S(1)} %get-tuple-element.56), channel_id=1, source_target_pairs={{0,6},{1,7},{2,4},{3,5},{4,2},{5,3},{6,0},{7,1},{8,14},{9,15},{10,... | collective-permute-start | bytes 122888 | tf_op jit(solution)/shard_map/ppermute | solution.py:191
  45.6 0.0 collective-permute-done.11
  45.6 0.4 collective-permute-done.15
  46.0 0.7 collective-permute-done.16
  46.7 2.7 %collective-permute-done.17 = f32[40,256]{1,0:T(8,128)S(1)} collective-permute-done((f32[40,256]{1,0:T(8,128)S(1)}, f32[40,256]{1,0:T(8,128)S(1)}, u32[]{:S(2)}, u32[]{:S(2)}) %collective-permute-start.17) | collective-permute-done | bytes 40992 | tf_op jit(solution)/shard_map/ppermute | solution.py:191
  49.4 1.1 %collective-permute-start.18 = (f32[40,256]{1,0:T(8,128)S(1)}, f32[40,256]{1,0:T(8,128)S(1)}, u32[]{:S(2)}, u32[]{:S(2)}) collective-permute-start(f32[40,256]{1,0:T(8,128)S(1)} %fusion), channel_id=1, source_target_pairs={{0,8},{8,0},{16,24},{24,16},{1,9},{9,1},{17,25},{25,17},{2,10},{10... | collective-permute-start | bytes 122888 | tf_op jit(solution)/shard_map/ppermute | solution.py:191
  50.4 1.2 %collective-permute-start.19 = (f32[40,256]{1,0:T(8,128)S(1)}, f32[40,256]{1,0:T(8,128)S(1)}, u32[]{:S(2)}, u32[]{:S(2)}) collective-permute-start(f32[40,256]{1,0:T(8,128)S(1)} %fusion), channel_id=1, source_target_pairs={{0,16},{8,24},{16,0},{24,8},{1,17},{9,25},{17,1},{25,9},{2,18},{10... | collective-permute-start | bytes 122888 | tf_op jit(solution)/shard_map/ppermute | solution.py:191
  51.6 1.3 %collective-permute-start.20 = (f32[40,256]{1,0:T(8,128)S(1)}, f32[40,256]{1,0:T(8,128)S(1)}, u32[]{:S(2)}, u32[]{:S(2)}) collective-permute-start(f32[40,256]{1,0:T(8,128)S(1)} %fusion), channel_id=1, source_target_pairs={{0,24},{8,16},{16,8},{24,0},{1,25},{9,17},{17,9},{25,1},{2,26},{10... | collective-permute-start | bytes 122888 | tf_op jit(solution)/shard_map/ppermute | solution.py:191
  52.9 0.0 collective-permute-done.12
  52.9 0.5 collective-permute-done.18
  53.4 1.0 %collective-permute-done.19 = f32[40,256]{1,0:T(8,128)S(1)} collective-permute-done((f32[40,256]{1,0:T(8,128)S(1)}, f32[40,256]{1,0:T(8,128)S(1)}, u32[]{:S(2)}, u32[]{:S(2)}) %collective-permute-start.19) | collective-permute-done | bytes 40992 | tf_op jit(solution)/shard_map/ppermute | solution.py:191
  54.4 2.1 %collective-permute-done.20 = f32[40,256]{1,0:T(8,128)S(1)} collective-permute-done((f32[40,256]{1,0:T(8,128)S(1)}, f32[40,256]{1,0:T(8,128)S(1)}, u32[]{:S(2)}, u32[]{:S(2)}) %collective-permute-start.20) | collective-permute-done | bytes 40992 | tf_op jit(solution)/shard_map/ppermute | solution.py:191
  56.5 0.1 collective-permute-start.21
  56.6 2.6 %collective-permute-start.22 = (f32[32,256]{1,0:T(8,128)S(1)}, f32[32,256]{1,0:T(8,128)S(1)}, u32[]{:S(2)}, u32[]{:S(2)}) collective-permute-start(f32[32,256]{1,0:T(8,128)S(1)} %slice.100), channel_id=1, source_target_pairs={{0,4},{1,5},{2,6},{3,7},{4,0},{5,1},{6,2},{7,3},{8,12},{9,13},{10,... | collective-permute-start | bytes 98312 | tf_op jit(solution)/shard_map/ppermute | solution.py:191
  59.2 1.8 %collective-permute-start.23 = (f32[32,256]{1,0:T(8,128)S(1)}, f32[32,256]{1,0:T(8,128)S(1)}, u32[]{:S(2)}, u32[]{:S(2)}) collective-permute-start(f32[32,256]{1,0:T(8,128)S(1)} %slice.100), channel_id=1, source_target_pairs={{0,6},{1,7},{2,4},{3,5},{4,2},{5,3},{6,0},{7,1},{8,14},{9,15},{10,... | collective-permute-start | bytes 98312 | tf_op jit(solution)/shard_map/ppermute | solution.py:191
  61.0 0.1 collective-permute-start.13
  61.1 0.0 collective-permute-done.21
  61.1 0.4 collective-permute-done.22
  61.5 3.4 %collective-permute-done.23 = f32[32,256]{1,0:T(8,128)S(1)} collective-permute-done((f32[32,256]{1,0:T(8,128)S(1)}, f32[32,256]{1,0:T(8,128)S(1)}, u32[]{:S(2)}, u32[]{:S(2)}) %collective-permute-start.23) | collective-permute-done | bytes 32800 | tf_op jit(solution)/shard_map/ppermute | solution.py:191
  64.9 0.1 collective-permute-start.24
  65.0 0.7 %shard_map.125 = f32[128,256]{1,0:T(8,128)} custom-call(f32[128,256]{1,0:T(8,128)S(1)} %get-tuple-element.43.pre_ref), custom_call_target="tpu_custom_call" | custom-call | bytes 262144 | tf_op jit(solution)/shard_map/pallas_call | solution.py:40
  65.7 0.0 collective-permute-done.13.partner_ref
  65.7 1.1 %shard_map.127 = f32[128,256]{1,0:T(8,128)} custom-call(s32[1,256]{1,0:T(1,128)S(1)} %get-tuple-element.44.wanted_ref, bf16[256,256]{1,0:T(8,128)(2,1)S(1)} %get-tuple-element.40.refs_4_.high_ref, bf16[256,256]{1,0:T(8,128)(2,1)S(1)} %get-tuple-element.41.refs_5_.low_ref, f32[128,256]{1,0:T(8,128)S(1)} %pad_maximum_fusion.2.own_ref, ...), custom_call_target="tpu_custom_call" | custom-call | flops 50331648 | bytes 656384 | tf_op jit(solution)/shard_map/pallas_call | solution.py:40
  66.8 0.0 collective-permute-done.24.partner_ref
  66.8 0.7 %shard_map.128 = (f32[256,256]{1,0:T(8,128)}, f32[1,256]{1,0:T(1,128)}) custom-call(f32[40,256]{1,0:T(8,128)S(1)} %add_add_fusion.summed_ref, f32[128,256]{1,0:T(8,128)S(1)} %pad_maximum_fusion.4.own_ref, f32[128,256]{1,0:T(8,128)S(1)} %collective-permute-done.24.partner_ref), custom_call_target="tpu_custom_call" | custom-call | bytes 566272 | tf_op jit(solution)/shard_map/pallas_call | solution.py:40
  (19 shorter events, 0.2 us)
Async XLA Ops:
  1.7 5.7 %collective-permute-start = (f32[64,256]{1,0:T(8,128)S(1)}, f32[64,256]{1,0:T(8,128)S(1)}, u32[]{:S(2)}, u32[]{:S(2)}) collective-permute-start(f32[64,256]{1,0:T(8,128)S(1)} %get-tuple-element.33), channel_id=1, source_target_pairs={{0,2},{1,3},{2,0},{3,1},{4,6},{5,7},{6,4},{7,5},{8,10},{9,11},{10,... | collective-permute-start | bytes 196616 | tf_op jit(solution)/shard_map/ppermute | solution.py:191
  4.9 7.3 %collective-permute-start.1 = (f32[64,256]{1,0:T(8,128)S(1)}, f32[64,256]{1,0:T(8,128)S(1)}, u32[]{:S(2)}, u32[]{:S(2)}) collective-permute-start(f32[64,256]{1,0:T(8,128)S(1)} %get-tuple-element.34), channel_id=1, source_target_pairs={{0,4},{1,5},{2,6},{3,7},{4,0},{5,1},{6,2},{7,3},{8,12},{9,13},{10,... | collective-permute-start | bytes 196616 | tf_op jit(solution)/shard_map/ppermute | solution.py:191
  7.5 6.1 %collective-permute-start.2 = (f32[64,256]{1,0:T(8,128)S(1)}, f32[64,256]{1,0:T(8,128)S(1)}, u32[]{:S(2)}, u32[]{:S(2)}) collective-permute-start(f32[64,256]{1,0:T(8,128)S(1)} %get-tuple-element.35), channel_id=1, source_target_pairs={{0,6},{1,7},{2,4},{3,5},{4,2},{5,3},{6,0},{7,1},{8,14},{9,15},{10,... | collective-permute-start | bytes 196616 | tf_op jit(solution)/shard_map/ppermute | solution.py:191
  13.6 2.8 %collective-permute-start.3 = (f32[128,256]{1,0:T(8,128)S(1)}, f32[128,256]{1,0:T(8,128)S(1)}, u32[]{:S(2)}, u32[]{:S(2)}) collective-permute-start(f32[128,256]{1,0:T(8,128)S(1)} %pad_maximum_fusion.1), channel_id=1, source_target_pairs={{0,1},{1,0},{2,3},{3,2},{4,5},{5,4},{6,7},{7,6},{8,9},{9,8},{10,11... | collective-permute-start | bytes 393224 | tf_op jit(solution)/shard_map/ppermute | solution.py:191
  16.3 4.0 %copy-start = (f32[256,256]{1,0:T(8,128)S(1)}, f32[256,256]{1,0:T(8,128)}, u32[]{:S(2)}) copy-start(f32[256,256]{1,0:T(8,128)} %weight_ref.1) | copy-start | bytes 786436
  16.7 6.4 %collective-permute-start.4 = (f32[128,256]{1,0:T(8,128)S(1)}, f32[128,256]{1,0:T(8,128)S(1)}, u32[]{:S(2)}, u32[]{:S(2)}) collective-permute-start(f32[128,256]{1,0:T(8,128)S(1)} %get-tuple-element.37), channel_id=1, source_target_pairs={{0,8},{8,0},{16,24},{24,16},{1,9},{9,1},{17,25},{25,17},{2,10},{10... | collective-permute-start | bytes 393224 | tf_op jit(solution)/shard_map/ppermute | solution.py:191
  18.3 8.4 %collective-permute-start.5 = (f32[128,256]{1,0:T(8,128)S(1)}, f32[128,256]{1,0:T(8,128)S(1)}, u32[]{:S(2)}, u32[]{:S(2)}) collective-permute-start(f32[128,256]{1,0:T(8,128)S(1)} %get-tuple-element.38), channel_id=1, source_target_pairs={{0,16},{8,24},{16,0},{24,8},{1,17},{9,25},{17,1},{25,9},{2,18},{10... | collective-permute-start | bytes 393224 | tf_op jit(solution)/shard_map/ppermute | solution.py:191
  19.8 0.7 %copy-start.2 = (f32[256]{0:T(256)S(1)}, f32[256]{0:T(256)}, u32[]{:S(2)}) copy-start(f32[256]{0:T(256)} %param.11) | copy-start | bytes 3076
  19.8 6.9 %collective-permute-start.6 = (f32[128,256]{1,0:T(8,128)S(1)}, f32[128,256]{1,0:T(8,128)S(1)}, u32[]{:S(2)}, u32[]{:S(2)}) collective-permute-start(f32[128,256]{1,0:T(8,128)S(1)} %get-tuple-element.39), channel_id=1, source_target_pairs={{0,24},{8,16},{16,8},{24,0},{1,25},{9,17},{17,9},{25,1},{2,26},{10... | collective-permute-start | bytes 393224 | tf_op jit(solution)/shard_map/ppermute | solution.py:191
  20.5 6.2 %copy-start.1 = (f32[128,256]{1,0:T(8,128)S(1)}, f32[128,256]{1,0:T(8,128)}, u32[]{:S(2)}) copy-start(f32[128,256]{1,0:T(8,128)} %refs_7_.1) | copy-start | bytes 393220
  27.3 5.6 %collective-permute-start.7 = (f32[128,256]{1,0:T(8,128)S(1)}, f32[128,256]{1,0:T(8,128)S(1)}, u32[]{:S(2)}, u32[]{:S(2)}) collective-permute-start(f32[128,256]{1,0:T(8,128)S(1)} %get-tuple-element.47.refs_0_), channel_id=1, source_target_pairs={{0,8},{8,0},{16,24},{24,16},{1,9},{9,1},{17,25},{25,17},{2,10},{10... | collective-permute-start | bytes 393224 | tf_op jit(solution)/shard_map/ppermute | solution.py:191
  28.6 7.6 %collective-permute-start.8 = (f32[128,256]{1,0:T(8,128)S(1)}, f32[128,256]{1,0:T(8,128)S(1)}, u32[]{:S(2)}, u32[]{:S(2)}) collective-permute-start(f32[128,256]{1,0:T(8,128)S(1)} %get-tuple-element.47.refs_0_), channel_id=1, source_target_pairs={{0,16},{8,24},{16,0},{24,8},{1,17},{9,25},{17,1},{25,9},{2,18},{10... | collective-permute-start | bytes 393224 | tf_op jit(solution)/shard_map/ppermute | solution.py:191
  29.5 6.7 %collective-permute-start.9 = (f32[128,256]{1,0:T(8,128)S(1)}, f32[128,256]{1,0:T(8,128)S(1)}, u32[]{:S(2)}, u32[]{:S(2)}) collective-permute-start(f32[128,256]{1,0:T(8,128)S(1)} %get-tuple-element.47.refs_0_), channel_id=1, source_target_pairs={{0,24},{8,16},{16,8},{24,0},{1,25},{9,17},{17,9},{25,1},{2,26},{10... | collective-permute-start | bytes 393224 | tf_op jit(solution)/shard_map/ppermute | solution.py:191
  30.9 10.2 %collective-permute-start.14 = (f32[160,256]{1,0:T(8,128)S(1)}, f32[160,256]{1,0:T(8,128)S(1)}, u32[]{:S(2)}, u32[]{:S(2)}) collective-permute-start(f32[160,256]{1,0:T(8,128)S(1)} %get-tuple-element.53), channel_id=1, source_target_pairs={{0,1},{1,0},{2,3},{3,2},{4,5},{5,4},{6,7},{7,6},{8,9},{9,8},{10,11... | collective-permute-start | bytes 491528 | tf_op jit(solution)/shard_map/ppermute | solution.py:191
  36.6 7.0 %collective-permute-start.10 = (f32[64,256]{1,0:T(8,128)S(1)}, f32[64,256]{1,0:T(8,128)S(1)}, u32[]{:S(2)}, u32[]{:S(2)}) collective-permute-start(f32[64,256]{1,0:T(8,128)S(1)} %get-tuple-element.49), channel_id=1, source_target_pairs={{0,2},{1,3},{2,0},{3,1},{4,6},{5,7},{6,4},{7,5},{8,10},{9,11},{10,... | collective-permute-start | bytes 196616 | tf_op jit(solution)/shard_map/ppermute | solution.py:191
  36.7 8.9 %collective-permute-start.11 = (f32[64,256]{1,0:T(8,128)S(1)}, f32[64,256]{1,0:T(8,128)S(1)}, u32[]{:S(2)}, u32[]{:S(2)}) collective-permute-start(f32[64,256]{1,0:T(8,128)S(1)} %get-tuple-element.50), channel_id=1, source_target_pairs={{0,4},{1,5},{2,6},{3,7},{4,0},{5,1},{6,2},{7,3},{8,12},{9,13},{10,... | collective-permute-start | bytes 196616 | tf_op jit(solution)/shard_map/ppermute | solution.py:191
  39.0 13.9 %collective-permute-start.12 = (f32[64,256]{1,0:T(8,128)S(1)}, f32[64,256]{1,0:T(8,128)S(1)}, u32[]{:S(2)}, u32[]{:S(2)}) collective-permute-start(f32[64,256]{1,0:T(8,128)S(1)} %get-tuple-element.51), channel_id=1, source_target_pairs={{0,6},{1,7},{2,4},{3,5},{4,2},{5,3},{6,0},{7,1},{8,14},{9,15},{10,... | collective-permute-start | bytes 196616 | tf_op jit(solution)/shard_map/ppermute | solution.py:191
  41.1 4.9 %collective-permute-start.15 = (f32[40,256]{1,0:T(8,128)S(1)}, f32[40,256]{1,0:T(8,128)S(1)}, u32[]{:S(2)}, u32[]{:S(2)}) collective-permute-start(f32[40,256]{1,0:T(8,128)S(1)} %get-tuple-element.58), channel_id=1, source_target_pairs={{0,2},{1,3},{2,0},{3,1},{4,6},{5,7},{6,4},{7,5},{8,10},{9,11},{10,... | collective-permute-start | bytes 122888 | tf_op jit(solution)/shard_map/ppermute | solution.py:191
  41.2 5.5 %collective-permute-start.16 = (f32[40,256]{1,0:T(8,128)S(1)}, f32[40,256]{1,0:T(8,128)S(1)}, u32[]{:S(2)}, u32[]{:S(2)}) collective-permute-start(f32[40,256]{1,0:T(8,128)S(1)} %get-tuple-element.57), channel_id=1, source_target_pairs={{0,4},{1,5},{2,6},{3,7},{4,0},{5,1},{6,2},{7,3},{8,12},{9,13},{10,... | collective-permute-start | bytes 122888 | tf_op jit(solution)/shard_map/ppermute | solution.py:191
  43.6 5.8 %collective-permute-start.17 = (f32[40,256]{1,0:T(8,128)S(1)}, f32[40,256]{1,0:T(8,128)S(1)}, u32[]{:S(2)}, u32[]{:S(2)}) collective-permute-start(f32[40,256]{1,0:T(8,128)S(1)} %get-tuple-element.56), channel_id=1, source_target_pairs={{0,6},{1,7},{2,4},{3,5},{4,2},{5,3},{6,0},{7,1},{8,14},{9,15},{10,... | collective-permute-start | bytes 122888 | tf_op jit(solution)/shard_map/ppermute | solution.py:191
  49.4 4.1 %collective-permute-start.18 = (f32[40,256]{1,0:T(8,128)S(1)}, f32[40,256]{1,0:T(8,128)S(1)}, u32[]{:S(2)}, u32[]{:S(2)}) collective-permute-start(f32[40,256]{1,0:T(8,128)S(1)} %fusion), channel_id=1, source_target_pairs={{0,8},{8,0},{16,24},{24,16},{1,9},{9,1},{17,25},{25,17},{2,10},{10... | collective-permute-start | bytes 122888 | tf_op jit(solution)/shard_map/ppermute | solution.py:191
  50.4 4.0 %collective-permute-start.19 = (f32[40,256]{1,0:T(8,128)S(1)}, f32[40,256]{1,0:T(8,128)S(1)}, u32[]{:S(2)}, u32[]{:S(2)}) collective-permute-start(f32[40,256]{1,0:T(8,128)S(1)} %fusion), channel_id=1, source_target_pairs={{0,16},{8,24},{16,0},{24,8},{1,17},{9,25},{17,1},{25,9},{2,18},{10... | collective-permute-start | bytes 122888 | tf_op jit(solution)/shard_map/ppermute | solution.py:191
  51.6 4.9 %collective-permute-start.20 = (f32[40,256]{1,0:T(8,128)S(1)}, f32[40,256]{1,0:T(8,128)S(1)}, u32[]{:S(2)}, u32[]{:S(2)}) collective-permute-start(f32[40,256]{1,0:T(8,128)S(1)} %fusion), channel_id=1, source_target_pairs={{0,24},{8,16},{16,8},{24,0},{1,25},{9,17},{17,9},{25,1},{2,26},{10... | collective-permute-start | bytes 122888 | tf_op jit(solution)/shard_map/ppermute | solution.py:191
  56.5 4.5 %collective-permute-start.21 = (f32[32,256]{1,0:T(8,128)S(1)}, f32[32,256]{1,0:T(8,128)S(1)}, u32[]{:S(2)}, u32[]{:S(2)}) collective-permute-start(f32[32,256]{1,0:T(8,128)S(1)} %slice.100), channel_id=1, source_target_pairs={{0,2},{1,3},{2,0},{3,1},{4,6},{5,7},{6,4},{7,5},{8,10},{9,11},{10,... | collective-permute-start | bytes 98312 | tf_op jit(solution)/shard_map/ppermute | solution.py:191
  56.6 4.9 %collective-permute-start.22 = (f32[32,256]{1,0:T(8,128)S(1)}, f32[32,256]{1,0:T(8,128)S(1)}, u32[]{:S(2)}, u32[]{:S(2)}) collective-permute-start(f32[32,256]{1,0:T(8,128)S(1)} %slice.100), channel_id=1, source_target_pairs={{0,4},{1,5},{2,6},{3,7},{4,0},{5,1},{6,2},{7,3},{8,12},{9,13},{10,... | collective-permute-start | bytes 98312 | tf_op jit(solution)/shard_map/ppermute | solution.py:191
  59.2 5.7 %collective-permute-start.23 = (f32[32,256]{1,0:T(8,128)S(1)}, f32[32,256]{1,0:T(8,128)S(1)}, u32[]{:S(2)}, u32[]{:S(2)}) collective-permute-start(f32[32,256]{1,0:T(8,128)S(1)} %slice.100), channel_id=1, source_target_pairs={{0,6},{1,7},{2,4},{3,5},{4,2},{5,3},{6,0},{7,1},{8,14},{9,15},{10,... | collective-permute-start | bytes 98312 | tf_op jit(solution)/shard_map/ppermute | solution.py:191
  61.0 4.7 %collective-permute-start.13 = (f32[128,256]{1,0:T(8,128)S(1)}, f32[128,256]{1,0:T(8,128)S(1)}, u32[]{:S(2)}, u32[]{:S(2)}) collective-permute-start(f32[128,256]{1,0:T(8,128)S(1)} %pad_maximum_fusion.3), channel_id=1, source_target_pairs={{0,1},{1,0},{2,3},{3,2},{4,5},{5,4},{6,7},{7,6},{8,9},{9,8},{10,11... | collective-permute-start | bytes 393224 | tf_op jit(solution)/shard_map/ppermute | solution.py:191
  64.9 1.9 %collective-permute-start.24 = (f32[128,256]{1,0:T(8,128)S(1)}, f32[128,256]{1,0:T(8,128)S(1)}, u32[]{:S(2)}, u32[]{:S(2)}) collective-permute-start(f32[128,256]{1,0:T(8,128)S(1)} %pad_maximum_fusion.4.own_ref), channel_id=1, source_target_pairs={{0,1},{1,0},{2,3},{3,2},{4,5},{5,4},{6,7},{7,6},{8,9},{9,8},{10,11... | collective-permute-start | bytes 393224 | tf_op jit(solution)/shard_map/ppermute | solution.py:191

commit v2 on v1

--- a/solution.py
+++ b/solution.py
@@ -25,12 +25,29 @@
     return high, (x - high.astype(F32)).astype(BF16)
 
 
+def split3(x):
+    high = x.astype(BF16)
+    rest = x - high.astype(F32)
+    middle = rest.astype(BF16)
+    return high, middle, (rest - middle.astype(F32)).astype(BF16)
+
+
 def mm(a, b, dims):
     return lax.dot_general(a, b, dims, preferred_element_type=F32)
 
 
 def mm3(a, b, dims):
     return mm(a[0], b[0], dims) + (mm(a[0], b[1], dims) + mm(a[1], b[0], dims))
+
+
+def mm6(a, b, dims):
+    small = mm(a[0], b[2], dims) + mm(a[1], b[1], dims) + mm(a[2], b[0], dims)
+    return mm(a[0], b[0], dims) + (mm(a[0], b[1], dims) + mm(a[1], b[0], dims) + small)
+
+
+def selected(pick, x):
+    high, middle, low = split3(x)
+    return mm(pick, high, NN) + (mm(pick, middle, NN) + mm(pick, low, NN))
 
 
 def call(kernel, outs, args, scratch=(), flops=0, smem=(), hbm=()):
@@ -108,12 +125,11 @@
     pick = one_hot(wanted_ref[...], feat_ref.shape[0]).T
     for copy in copies:
         copy.wait()
-    high, low = split(feat_ref[...])
-    buffer[...] = mm(pick, high, NN) + mm(pick, low, NN)
+    buffer[...] = selected(pick, feat_ref[...])
     put_pairs(outs, buffer, me, outs[0].shape[0] // 2)
 
 
-def aggregate(pairs, high_ref, low_ref, own_ref, partner_ref, *outs):
+def aggregate(pairs, high_ref, middle_ref, low_ref, own_ref, partner_ref, *outs):
     per = own_ref.shape[0] // pairs
     same = lax.axis_index("row") % 2 == 0
     own, partner = own_ref[...], partner_ref[...]
@@ -123,18 +139,20 @@
         for half in (lower, upper):
             pieces.append(half[pair * per : (pair + 1) * per, :])
     border = jnp.concatenate(pieces, axis=0)
-    result = mm3((high_ref[...], low_ref[...]), split(border), NN)
+    dense = high_ref[...], middle_ref[...], low_ref[...]
+    result = mm6(dense, split3(border), NN)
     for s, out in enumerate(outs):
         out[...] = result[s * out.shape[0] : (s + 1) * out.shape[0], :]
 
 
 def activate(groups, members, *refs):
     pieces = refs[:groups]
-    high_ref, low_ref, bias_ref, cot_ref, pre_ref, grad_ref, keep_ref, send_ref, buffer = refs[groups:]
+    high_ref, middle_ref, low_ref, bias_ref, cot_ref, pre_ref, grad_ref, keep_ref, send_ref, buffer = refs[groups:]
     me = lax.axis_index("row")
     total = tree_sum([piece[...] for piece in pieces])
-    total_split = split(total)
-    pre = mm3(total_split, (high_ref[...], low_ref[...]), NN) + bias_ref[...]
+    total_split = split3(total)
+    weight = high_ref[...], middle_ref[...], low_ref[...]
+    pre = mm6(total_split, weight, NN) + bias_ref[...]
     gate = jax.nn.sigmoid(pre)
     pre_ref[...] = pre
     grad = cot_ref[...] * (gate * (1.0 + pre * (1.0 - gate)))
@@ -229,7 +247,7 @@
     bias_row = jax.ShapeDtypeStruct((1, width), F32)
     dense = call(
         functools.partial(build, nodes // BS),
-        [wide, wide],
+        [wide, wide, wide],
         [
             live_blocks,
             *(
@@ -254,8 +272,10 @@
         flops=6 * rows * slots * width,
     )
     half_weight = jax.ShapeDtypeStruct(weight.shape, BF16)
-    *turned, bias_here, weight_high, weight_low = call(
-        prepare, [tall, tall, bias_row, half_weight, half_weight], [*dense, bias[None, :], weight]
+    *turned, bias_here, weight_high, weight_middle, weight_low = call(
+        prepare,
+        [tall, tall, bias_row] + [half_weight] * 3,
+        [*dense[:2], bias[None, :], weight],
     )
     parts = [partials[0]] + [exchange(partials[s], "rep", s) for s in range(1, groups)]
     chunk = width // members
@@ -263,7 +283,7 @@
     pre, grad, keep, send = call(
         functools.partial(activate, groups, members),
         [shape(nodes), shape(nodes), shape(padded), shape(padded)],
-        parts + [weight_high, weight_low, bias_here, cotangent],
+        parts + [weight_high, weight_middle, weight_low, bias_here, cotangent],
         [vmem(width)],
         flops=12 * nodes * width * width,
     )
@@ -279,7 +299,7 @@
     (feat_grad,) = call(
         functools.partial(collect, per),
         [shape(nodes)],
-        [wanted, weight_high, weight_low] + returned,
+        [wanted, weight_high, weight_middle] + returned,
         [vmem(slots)],
         flops=6 * nodes * width * width,
     )
@@ -301,8 +321,8 @@
     return (activated, feat_grad, weight_grad, bias_grad[0])
 
 
-def build(shard_blocks, live_ref, rows_hbm, cols_hbm, blocks_hbm, high_ref, low_ref, *refs):
-    rows_ref, cols_ref, blocks_ref, dense, sems = refs
+def build(shard_blocks, live_ref, rows_hbm, cols_hbm, blocks_hbm, *refs):
+    high_ref, middle_ref, low_ref, rows_ref, cols_ref, blocks_ref, dense, sems = refs
     places = [
         pltpu.make_async_copy(rows_hbm, rows_ref, sems.at[PARTS]),
         pltpu.make_async_copy(cols_hbm, cols_ref, sems.at[PARTS + 1]),
@@ -324,8 +344,7 @@
     pick = ((pair == cols * row_blocks + rows) & (slot < live_ref[...])).astype(BF16)
     for copy in copies:
         copy.wait()
-    high, low = split(blocks_ref[...])
-    product = mm(pick, high, NN) + mm(pick, low, NN)
+    product = selected(pick, blocks_ref[...])
     left = lax.broadcasted_iota(jnp.int32, (row_blocks, LANES), 1) < BS
     for t in range(blocks_ref.shape[1] // LANES):
         lanes = slice(t * LANES, (t + 1) * LANES)
@@ -338,15 +357,15 @@
                 dense[u, pl.ds(2 * t + parity, row_blocks, stride=BS), :] = value
     for u in range(col_blocks // 2):
         lanes = slice(u * LANES, (u + 1) * LANES)
-        high_ref[:, lanes], low_ref[:, lanes] = split(dense[u])
+        high_ref[:, lanes], middle_ref[:, lanes], low_ref[:, lanes] = split3(dense[u])
 
 
 def prepare(high_ref, low_ref, bias_ref, weight_ref, *refs):
-    high_t_ref, low_t_ref, bias_out, weight_high, weight_low = refs
+    high_t_ref, low_t_ref, bias_out, weight_high, weight_middle, weight_low = refs
     high_t_ref[...] = high_ref[...].astype(F32).T.astype(BF16)
     low_t_ref[...] = low_ref[...].astype(F32).T.astype(BF16)
     bias_out[...] = bias_ref[...]
-    weight_high[...], weight_low[...] = split(weight_ref[...])
+    weight_high[...], weight_middle[...], weight_low[...] = split3(weight_ref[...])
 
 
 def solution(mesh):

time: 67.8 us -> 67 us (0.988)
  waiting for transfers between devices: 28.5 us -> 27 us
  Pallas kernels: 7.23 us -> 7.94 us
    ppermute x25, waiting for transfers between devices: 28.5 us -> 27 us  [exchange(): return lax.ppermute(value, axis, [(i, i ^ shift) for i in range(size)])]
    pallas_call x9, Pallas kernels: 7.23 us -> 7.94 us  [call(): pl.pallas_call(kernel, out_shape=outs, in_specs=[pl.BlockSpec(memory_spac...]
  transfers between devices with their start and end apart: 25 -> 25, of which waited for: 14 -> 15; matrix products, arithmetic and copies ran while one was open for 0% -> 0% of each run, Pallas kernels for 7% -> 7%
where the time goes in v2:
time: 67 us; the launch traced here: 66.8 us
  starting transfers between devices  29.9 us (45%)
  waiting for transfers between devices  27 us (40%)
  Pallas kernels  7.94 us (12%)
  between operations  1.48 us (2%)
    ppermute x25, starting transfers between devices, exchange(): return lax.ppermute(value, axis, [(i, i ^ shift) for i in range(size)])  29.9 us
    ppermute x25, waiting for transfers between devices, exchange(): return lax.ppermute(value, axis, [(i, i ^ shift) for i in range(size)])  27 us
    pallas_call x9, Pallas kernels, call(): pl.pallas_call(kernel, out_shape=outs, in_specs=[pl.BlockSpec(memory_spac...  7.94 us
  transfers between devices with their start and end apart: 25, of which 15 were waited for; matrix products, arithmetic and copies ran while one was open for 0% of the time, Pallas kernels for 7%

profile of v2, /device:TPU:0, one launch (start us, length us, event | category | flops | bytes accessed | tf_op | source)
XLA Modules:
  0.0 66.8 jit_solution(6995642919914161939)
XLA Ops:
  0.6 1.2 %shard_map.121 = (f32[64,256]{1,0:T(8,128)S(1)}, f32[64,256]{1,0:T(8,128)S(1)}, f32[64,256]{1,0:T(8,128)S(1)}, f32[64,256]{1,0:T(8,128)S(1)}, s32[1,256]{1,0:T(1,128)S(1)}) custom-call(s32[1,2048]{1,0:T(1,128)} %list_hbm.1, f32[128,256]{1,0:T(8,128)} %feat_hbm.1), custom_call_target="tpu_custom_call" | custom-call | bytes 402432 | tf_op jit(solution)/shard_map/pallas_call | solution.py:57
  1.8 3.1 %collective-permute-start = (f32[64,256]{1,0:T(8,128)S(1)}, f32[64,256]{1,0:T(8,128)S(1)}, u32[]{:S(2)}, u32[]{:S(2)}) collective-permute-start(f32[64,256]{1,0:T(8,128)S(1)} %get-tuple-element.36), channel_id=1, source_target_pairs={{0,2},{1,3},{2,0},{3,1},{4,6},{5,7},{6,4},{7,5},{8,10},{9,11},{10,... | collective-permute-start | bytes 196616 | tf_op jit(solution)/shard_map/ppermute | solution.py:209
  4.9 2.6 %collective-permute-start.1 = (f32[64,256]{1,0:T(8,128)S(1)}, f32[64,256]{1,0:T(8,128)S(1)}, u32[]{:S(2)}, u32[]{:S(2)}) collective-permute-start(f32[64,256]{1,0:T(8,128)S(1)} %get-tuple-element.37), channel_id=1, source_target_pairs={{0,4},{1,5},{2,6},{3,7},{4,0},{5,1},{6,2},{7,3},{8,12},{9,13},{10,... | collective-permute-start | bytes 196616 | tf_op jit(solution)/shard_map/ppermute | solution.py:209
  7.5 0.0 collective-permute-start.2
  7.5 0.0 collective-permute-done
  7.5 4.6 %collective-permute-done.1 = f32[64,256]{1,0:T(8,128)S(1)} collective-permute-done((f32[64,256]{1,0:T(8,128)S(1)}, f32[64,256]{1,0:T(8,128)S(1)}, u32[]{:S(2)}, u32[]{:S(2)}) %collective-permute-start.1) | collective-permute-done | bytes 65568 | tf_op jit(solution)/shard_map/ppermute | solution.py:209
  12.2 1.4 %collective-permute-done.2 = f32[64,256]{1,0:T(8,128)S(1)} collective-permute-done((f32[64,256]{1,0:T(8,128)S(1)}, f32[64,256]{1,0:T(8,128)S(1)}, u32[]{:S(2)}, u32[]{:S(2)}) %collective-permute-start.2) | collective-permute-done | bytes 65568 | tf_op jit(solution)/shard_map/ppermute | solution.py:209
  13.6 0.1 collective-permute-start.3
  14.3 2.3 %shard_map.120 = (bf16[512,256]{1,0:T(8,128)(2,1)S(1)}, bf16[512,256]{1,0:T(8,128)(2,1)S(1)}, bf16[512,256]{1,0:T(8,128)(2,1)S(1)}) custom-call(s32[1,1]{1,0:T(1,128)S(6)} %copy.13.live_ref, s32[1,64]{1,0:T(1,128)} %bitcast.7, s32[1,64]{1,0:T(1,128)} %bitcast.8, f32[64,4096]{1,0:T(8,128)} %bitcast.6), custom_call_target="tpu_custom_call" | custom-call | flops 33554432 | bytes 1835524 | tf_op jit(solution)/shard_map/pallas_call | solution.py:57
  16.6 0.0 collective-permute-done.3.partner_ref
  16.7 0.0 copy-start
  16.7 0.6 shard_map.122
  17.3 1.6 %collective-permute-start.4 = (f32[128,256]{1,0:T(8,128)S(1)}, f32[128,256]{1,0:T(8,128)S(1)}, u32[]{:S(2)}, u32[]{:S(2)}) collective-permute-start(f32[128,256]{1,0:T(8,128)S(1)} %get-tuple-element.40), channel_id=1, source_target_pairs={{0,8},{8,0},{16,24},{24,16},{1,9},{9,1},{17,25},{25,17},{2,10},{10... | collective-permute-start | bytes 393224 | tf_op jit(solution)/shard_map/ppermute | solution.py:209
  18.8 1.5 %collective-permute-start.5 = (f32[128,256]{1,0:T(8,128)S(1)}, f32[128,256]{1,0:T(8,128)S(1)}, u32[]{:S(2)}, u32[]{:S(2)}) collective-permute-start(f32[128,256]{1,0:T(8,128)S(1)} %get-tuple-element.41), channel_id=1, source_target_pairs={{0,16},{8,24},{16,0},{24,8},{1,17},{9,25},{17,1},{25,9},{2,18},{10... | collective-permute-start | bytes 393224 | tf_op jit(solution)/shard_map/ppermute | solution.py:209
  20.3 0.0 copy-start.2
  20.4 0.5 collective-permute-start.6
  20.8 0.0 copy-done
  20.8 0.2 copy-done.2
  21.0 0.3 shard_map.123
  21.3 2.3 %collective-permute-done.4.refs_1_ = f32[128,256]{1,0:T(8,128)S(1)} collective-permute-done((f32[128,256]{1,0:T(8,128)S(1)}, f32[128,256]{1,0:T(8,128)S(1)}, u32[]{:S(2)}, u32[]{:S(2)}) %collective-permute-start.4) | collective-permute-done | bytes 131104 | tf_op jit(solution)/shard_map/ppermute | solution.py:209
  23.6 3.6 %collective-permute-done.5.refs_2_ = f32[128,256]{1,0:T(8,128)S(1)} collective-permute-done((f32[128,256]{1,0:T(8,128)S(1)}, f32[128,256]{1,0:T(8,128)S(1)}, u32[]{:S(2)}, u32[]{:S(2)}) %collective-permute-start.5) | collective-permute-done | bytes 131104 | tf_op jit(solution)/shard_map/ppermute | solution.py:209
  27.3 0.0 collective-permute-done.6.refs_3_
  27.3 0.0 copy-done.1
  27.3 0.7 %shard_map.124 = (f32[128,256]{1,0:T(8,128)S(1)}, f32[128,256]{1,0:T(8,128)S(1)}, f32[160,256]{1,0:T(8,128)S(1)}, f32[160,256]{1,0:T(8,128)S(1)}) custom-call(f32[128,256]{1,0:T(8,128)S(1)} %get-tuple-element.39.refs_0_, f32[128,256]{1,0:T(8,128)S(1)} %collective-permute-done.4.refs_1_, f32[128,256]{1,0:T(8,128)S(1)} %collective-permute-done.5.refs_2_, ...), custom_call_target="tpu_custom_call" | custom-call | flops 100663296 | bytes 1639424 | tf_op jit(solution)/shard_map/pallas_call | solution.py:57
  28.0 1.6 %collective-permute-start.9 = (f32[128,256]{1,0:T(8,128)S(1)}, f32[128,256]{1,0:T(8,128)S(1)}, u32[]{:S(2)}, u32[]{:S(2)}) collective-permute-start(f32[128,256]{1,0:T(8,128)S(1)} %get-tuple-element.51.refs_0_), channel_id=1, source_target_pairs={{0,24},{8,16},{16,8},{24,0},{1,25},{9,17},{17,9},{25,1},{2,26},{10... | collective-permute-start | bytes 393224 | tf_op jit(solution)/shard_map/ppermute | solution.py:209
  29.6 1.2 %collective-permute-start.8 = (f32[128,256]{1,0:T(8,128)S(1)}, f32[128,256]{1,0:T(8,128)S(1)}, u32[]{:S(2)}, u32[]{:S(2)}) collective-permute-start(f32[128,256]{1,0:T(8,128)S(1)} %get-tuple-element.51.refs_0_), channel_id=1, source_target_pairs={{0,16},{8,24},{16,0},{24,8},{1,17},{9,25},{17,1},{25,9},{2,18},{10... | collective-permute-start | bytes 393224 | tf_op jit(solution)/shard_map/ppermute | solution.py:209
  30.7 0.8 %collective-permute-start.7 = (f32[128,256]{1,0:T(8,128)S(1)}, f32[128,256]{1,0:T(8,128)S(1)}, u32[]{:S(2)}, u32[]{:S(2)}) collective-permute-start(f32[128,256]{1,0:T(8,128)S(1)} %get-tuple-element.51.refs_0_), channel_id=1, source_target_pairs={{0,8},{8,0},{16,24},{24,16},{1,9},{9,1},{17,25},{25,17},{2,10},{10... | collective-permute-start | bytes 393224 | tf_op jit(solution)/shard_map/ppermute | solution.py:209
  31.6 0.0 collective-permute-start.14
  31.6 3.7 %collective-permute-done.9.refs_3_ = f32[128,256]{1,0:T(8,128)S(1)} collective-permute-done((f32[128,256]{1,0:T(8,128)S(1)}, f32[128,256]{1,0:T(8,128)S(1)}, u32[]{:S(2)}, u32[]{:S(2)}) %collective-permute-start.9) | collective-permute-done | bytes 131104 | tf_op jit(solution)/shard_map/ppermute | solution.py:209
  35.2 1.2 %collective-permute-done.8.refs_2_ = f32[128,256]{1,0:T(8,128)S(1)} collective-permute-done((f32[128,256]{1,0:T(8,128)S(1)}, f32[128,256]{1,0:T(8,128)S(1)}, u32[]{:S(2)}, u32[]{:S(2)}) %collective-permute-start.8) | collective-permute-done | bytes 131104 | tf_op jit(solution)/shard_map/ppermute | solution.py:209
  36.5 0.2 collective-permute-done.7.refs_1_
  36.6 0.4 shard_map.126
  37.0 0.1 collective-permute-start.10
  37.1 2.4 %collective-permute-start.11 = (f32[64,256]{1,0:T(8,128)S(1)}, f32[64,256]{1,0:T(8,128)S(1)}, u32[]{:S(2)}, u32[]{:S(2)}) collective-permute-start(f32[64,256]{1,0:T(8,128)S(1)} %get-tuple-element.54), channel_id=1, source_target_pairs={{0,4},{1,5},{2,6},{3,7},{4,0},{5,1},{6,2},{7,3},{8,12},{9,13},{10,... | collective-permute-start | bytes 196616 | tf_op jit(solution)/shard_map/ppermute | solution.py:209
  39.5 2.0 %collective-permute-start.12 = (f32[64,256]{1,0:T(8,128)S(1)}, f32[64,256]{1,0:T(8,128)S(1)}, u32[]{:S(2)}, u32[]{:S(2)}) collective-permute-start(f32[64,256]{1,0:T(8,128)S(1)} %get-tuple-element.55), channel_id=1, source_target_pairs={{0,6},{1,7},{2,4},{3,5},{4,2},{5,3},{6,0},{7,1},{8,14},{9,15},{10,... | collective-permute-start | bytes 196616 | tf_op jit(solution)/shard_map/ppermute | solution.py:209
  41.5 0.0 collective-permute-done.14
  41.5 1.9 %collective-permute-start.17 = (f32[40,256]{1,0:T(8,128)S(1)}, f32[40,256]{1,0:T(8,128)S(1)}, u32[]{:S(2)}, u32[]{:S(2)}) collective-permute-start(f32[40,256]{1,0:T(8,128)S(1)} %get-tuple-element.60), channel_id=1, source_target_pairs={{0,6},{1,7},{2,4},{3,5},{4,2},{5,3},{6,0},{7,1},{8,14},{9,15},{10,... | collective-permute-start | bytes 122888 | tf_op jit(solution)/shard_map/ppermute | solution.py:209
  43.4 0.0 collective-permute-start.16
  43.4 0.0 collective-permute-done.10
  43.4 2.6 %collective-permute-start.15 = (f32[40,256]{1,0:T(8,128)S(1)}, f32[40,256]{1,0:T(8,128)S(1)}, u32[]{:S(2)}, u32[]{:S(2)}) collective-permute-start(f32[40,256]{1,0:T(8,128)S(1)} %get-tuple-element.62), channel_id=1, source_target_pairs={{0,2},{1,3},{2,0},{3,1},{4,6},{5,7},{6,4},{7,5},{8,10},{9,11},{10,... | collective-permute-start | bytes 122888 | tf_op jit(solution)/shard_map/ppermute | solution.py:209
  46.0 0.2 collective-permute-done.11
  46.2 1.3 %collective-permute-done.17 = f32[40,256]{1,0:T(8,128)S(1)} collective-permute-done((f32[40,256]{1,0:T(8,128)S(1)}, f32[40,256]{1,0:T(8,128)S(1)}, u32[]{:S(2)}, u32[]{:S(2)}) %collective-permute-start.17) | collective-permute-done | bytes 40992 | tf_op jit(solution)/shard_map/ppermute | solution.py:209
  47.5 2.0 %collective-permute-done.16 = f32[40,256]{1,0:T(8,128)S(1)} collective-permute-done((f32[40,256]{1,0:T(8,128)S(1)}, f32[40,256]{1,0:T(8,128)S(1)}, u32[]{:S(2)}, u32[]{:S(2)}) %collective-permute-start.16) | collective-permute-done | bytes 40992 | tf_op jit(solution)/shard_map/ppermute | solution.py:209
  49.5 0.0 collective-permute-done.15
  49.6 1.8 %collective-permute-start.20 = (f32[40,256]{1,0:T(8,128)S(1)}, f32[40,256]{1,0:T(8,128)S(1)}, u32[]{:S(2)}, u32[]{:S(2)}) collective-permute-start(f32[40,256]{1,0:T(8,128)S(1)} %fusion), channel_id=1, source_target_pairs={{0,24},{8,16},{16,8},{24,0},{1,25},{9,17},{17,9},{25,1},{2,26},{10... | collective-permute-start | bytes 122888 | tf_op jit(solution)/shard_map/ppermute | solution.py:209
  51.4 1.5 %collective-permute-start.19 = (f32[40,256]{1,0:T(8,128)S(1)}, f32[40,256]{1,0:T(8,128)S(1)}, u32[]{:S(2)}, u32[]{:S(2)}) collective-permute-start(f32[40,256]{1,0:T(8,128)S(1)} %fusion), channel_id=1, source_target_pairs={{0,16},{8,24},{16,0},{24,8},{1,17},{9,25},{17,1},{25,9},{2,18},{10... | collective-permute-start | bytes 122888 | tf_op jit(solution)/shard_map/ppermute | solution.py:209
  52.9 0.2 collective-permute-start.18
  53.1 0.0 collective-permute-done.12
  53.1 1.8 %collective-permute-done.20 = f32[40,256]{1,0:T(8,128)S(1)} collective-permute-done((f32[40,256]{1,0:T(8,128)S(1)}, f32[40,256]{1,0:T(8,128)S(1)}, u32[]{:S(2)}, u32[]{:S(2)}) %collective-permute-start.20) | collective-permute-done | bytes 40992 | tf_op jit(solution)/shard_map/ppermute | solution.py:209
  54.9 0.4 collective-permute-done.19
  55.4 1.5 %collective-permute-done.18 = f32[40,256]{1,0:T(8,128)S(1)} collective-permute-done((f32[40,256]{1,0:T(8,128)S(1)}, f32[40,256]{1,0:T(8,128)S(1)}, u32[]{:S(2)}, u32[]{:S(2)}) %collective-permute-start.18) | collective-permute-done | bytes 40992 | tf_op jit(solution)/shard_map/ppermute | solution.py:209
  56.9 2.4 %collective-permute-start.23 = (f32[32,256]{1,0:T(8,128)S(1)}, f32[32,256]{1,0:T(8,128)S(1)}, u32[]{:S(2)}, u32[]{:S(2)}) collective-permute-start(f32[32,256]{1,0:T(8,128)S(1)} %slice.100), channel_id=1, source_target_pairs={{0,6},{1,7},{2,4},{3,5},{4,2},{5,3},{6,0},{7,1},{8,14},{9,15},{10,... | collective-permute-start | bytes 98312 | tf_op jit(solution)/shard_map/ppermute | solution.py:209
  59.3 0.0 collective-permute-start.22
  59.3 2.1 %collective-permute-start.21 = (f32[32,256]{1,0:T(8,128)S(1)}, f32[32,256]{1,0:T(8,128)S(1)}, u32[]{:S(2)}, u32[]{:S(2)}) collective-permute-start(f32[32,256]{1,0:T(8,128)S(1)} %slice.100), channel_id=1, source_target_pairs={{0,2},{1,3},{2,0},{3,1},{4,6},{5,7},{6,4},{7,5},{8,10},{9,11},{10,... | collective-permute-start | bytes 98312 | tf_op jit(solution)/shard_map/ppermute | solution.py:209
  61.4 0.1 collective-permute-start.13
  61.5 1.2 %collective-permute-done.23 = f32[32,256]{1,0:T(8,128)S(1)} collective-permute-done((f32[32,256]{1,0:T(8,128)S(1)}, f32[32,256]{1,0:T(8,128)S(1)}, u32[]{:S(2)}, u32[]{:S(2)}) %collective-permute-start.23) | collective-permute-done | bytes 32800 | tf_op jit(solution)/shard_map/ppermute | solution.py:209
  62.7 1.4 %collective-permute-done.22 = f32[32,256]{1,0:T(8,128)S(1)} collective-permute-done((f32[32,256]{1,0:T(8,128)S(1)}, f32[32,256]{1,0:T(8,128)S(1)}, u32[]{:S(2)}, u32[]{:S(2)}) %collective-permute-start.22) | collective-permute-done | bytes 32800 | tf_op jit(solution)/shard_map/ppermute | solution.py:209
  64.1 0.0 collective-permute-done.21
  64.1 0.1 collective-permute-start.24
  64.2 0.7 %shard_map.125 = f32[128,256]{1,0:T(8,128)} custom-call(f32[128,256]{1,0:T(8,128)S(1)} %get-tuple-element.47.pre_ref), custom_call_target="tpu_custom_call" | custom-call | bytes 262144 | tf_op jit(solution)/shard_map/pallas_call | solution.py:57
  64.9 0.0 collective-permute-done.13.partner_ref
  64.9 1.1 %shard_map.127 = f32[128,256]{1,0:T(8,128)} custom-call(s32[1,256]{1,0:T(1,128)S(1)} %get-tuple-element.48.wanted_ref, bf16[256,256]{1,0:T(8,128)(2,1)S(1)} %get-tuple-element.43.refs_4_.high_ref, bf16[256,256]{1,0:T(8,128)(2,1)S(1)} %get-tuple-element.44.refs_5_.low_ref, f32[128,256]{1,0:T(8,128)S(1)} %pad_maximum_fusion.2.own_ref, ...), custom_call_target="tpu_custom_call" | custom-call | flops 50331648 | bytes 656384 | tf_op jit(solution)/shard_map/pallas_call | solution.py:57
  66.0 0.0 collective-permute-done.24.partner_ref
  66.0 0.7 %shard_map.128 = (f32[256,256]{1,0:T(8,128)}, f32[1,256]{1,0:T(1,128)}) custom-call(f32[40,256]{1,0:T(8,128)S(1)} %add_add_fusion.summed_ref, f32[128,256]{1,0:T(8,128)S(1)} %pad_maximum_fusion.4.own_ref, f32[128,256]{1,0:T(8,128)S(1)} %collective-permute-done.24.partner_ref), custom_call_target="tpu_custom_call" | custom-call | bytes 566272 | tf_op jit(solution)/shard_map/pallas_call | solution.py:57
  (19 shorter events, 0.2 us)
Async XLA Ops:
  1.8 5.7 %collective-permute-start = (f32[64,256]{1,0:T(8,128)S(1)}, f32[64,256]{1,0:T(8,128)S(1)}, u32[]{:S(2)}, u32[]{:S(2)}) collective-permute-start(f32[64,256]{1,0:T(8,128)S(1)} %get-tuple-element.36), channel_id=1, source_target_pairs={{0,2},{1,3},{2,0},{3,1},{4,6},{5,7},{6,4},{7,5},{8,10},{9,11},{10,... | collective-permute-start | bytes 196616 | tf_op jit(solution)/shard_map/ppermute | solution.py:209
  4.9 7.3 %collective-permute-start.1 = (f32[64,256]{1,0:T(8,128)S(1)}, f32[64,256]{1,0:T(8,128)S(1)}, u32[]{:S(2)}, u32[]{:S(2)}) collective-permute-start(f32[64,256]{1,0:T(8,128)S(1)} %get-tuple-element.37), channel_id=1, source_target_pairs={{0,4},{1,5},{2,6},{3,7},{4,0},{5,1},{6,2},{7,3},{8,12},{9,13},{10,... | collective-permute-start | bytes 196616 | tf_op jit(solution)/shard_map/ppermute | solution.py:209
  7.5 6.1 %collective-permute-start.2 = (f32[64,256]{1,0:T(8,128)S(1)}, f32[64,256]{1,0:T(8,128)S(1)}, u32[]{:S(2)}, u32[]{:S(2)}) collective-permute-start(f32[64,256]{1,0:T(8,128)S(1)} %get-tuple-element.38), channel_id=1, source_target_pairs={{0,6},{1,7},{2,4},{3,5},{4,2},{5,3},{6,0},{7,1},{8,14},{9,15},{10,... | collective-permute-start | bytes 196616 | tf_op jit(solution)/shard_map/ppermute | solution.py:209
  13.6 3.1 %collective-permute-start.3 = (f32[128,256]{1,0:T(8,128)S(1)}, f32[128,256]{1,0:T(8,128)S(1)}, u32[]{:S(2)}, u32[]{:S(2)}) collective-permute-start(f32[128,256]{1,0:T(8,128)S(1)} %pad_maximum_fusion.1), channel_id=1, source_target_pairs={{0,1},{1,0},{2,3},{3,2},{4,5},{5,4},{6,7},{7,6},{8,9},{9,8},{10,11... | collective-permute-start | bytes 393224 | tf_op jit(solution)/shard_map/ppermute | solution.py:209
  16.7 4.2 %copy-start = (f32[256,256]{1,0:T(8,128)S(1)}, f32[256,256]{1,0:T(8,128)}, u32[]{:S(2)}) copy-start(f32[256,256]{1,0:T(8,128)} %weight_ref.1) | copy-start | bytes 786436
  17.3 6.4 %collective-permute-start.4 = (f32[128,256]{1,0:T(8,128)S(1)}, f32[128,256]{1,0:T(8,128)S(1)}, u32[]{:S(2)}, u32[]{:S(2)}) collective-permute-start(f32[128,256]{1,0:T(8,128)S(1)} %get-tuple-element.40), channel_id=1, source_target_pairs={{0,8},{8,0},{16,24},{24,16},{1,9},{9,1},{17,25},{25,17},{2,10},{10... | collective-permute-start | bytes 393224 | tf_op jit(solution)/shard_map/ppermute | solution.py:209
  18.8 8.4 %collective-permute-start.5 = (f32[128,256]{1,0:T(8,128)S(1)}, f32[128,256]{1,0:T(8,128)S(1)}, u32[]{:S(2)}, u32[]{:S(2)}) collective-permute-start(f32[128,256]{1,0:T(8,128)S(1)} %get-tuple-element.41), channel_id=1, source_target_pairs={{0,16},{8,24},{16,0},{24,8},{1,17},{9,25},{17,1},{25,9},{2,18},{10... | collective-permute-start | bytes 393224 | tf_op jit(solution)/shard_map/ppermute | solution.py:209
  20.3 0.7 %copy-start.2 = (f32[256]{0:T(256)S(1)}, f32[256]{0:T(256)}, u32[]{:S(2)}) copy-start(f32[256]{0:T(256)} %param.11) | copy-start | bytes 3076
  20.4 6.9 %collective-permute-start.6 = (f32[128,256]{1,0:T(8,128)S(1)}, f32[128,256]{1,0:T(8,128)S(1)}, u32[]{:S(2)}, u32[]{:S(2)}) collective-permute-start(f32[128,256]{1,0:T(8,128)S(1)} %get-tuple-element.42), channel_id=1, source_target_pairs={{0,24},{8,16},{16,8},{24,0},{1,25},{9,17},{17,9},{25,1},{2,26},{10... | collective-permute-start | bytes 393224 | tf_op jit(solution)/shard_map/ppermute | solution.py:209
  21.0 6.2 %copy-start.1 = (f32[128,256]{1,0:T(8,128)S(1)}, f32[128,256]{1,0:T(8,128)}, u32[]{:S(2)}) copy-start(f32[128,256]{1,0:T(8,128)} %refs_8_.1) | copy-start | bytes 393220
  28.0 7.2 %collective-permute-start.9 = (f32[128,256]{1,0:T(8,128)S(1)}, f32[128,256]{1,0:T(8,128)S(1)}, u32[]{:S(2)}, u32[]{:S(2)}) collective-permute-start(f32[128,256]{1,0:T(8,128)S(1)} %get-tuple-element.51.refs_0_), channel_id=1, source_target_pairs={{0,24},{8,16},{16,8},{24,0},{1,25},{9,17},{17,9},{25,1},{2,26},{10... | collective-permute-start | bytes 393224 | tf_op jit(solution)/shard_map/ppermute | solution.py:209
  29.6 6.9 %collective-permute-start.8 = (f32[128,256]{1,0:T(8,128)S(1)}, f32[128,256]{1,0:T(8,128)S(1)}, u32[]{:S(2)}, u32[]{:S(2)}) collective-permute-start(f32[128,256]{1,0:T(8,128)S(1)} %get-tuple-element.51.refs_0_), channel_id=1, source_target_pairs={{0,16},{8,24},{16,0},{24,8},{1,17},{9,25},{17,1},{25,9},{2,18},{10... | collective-permute-start | bytes 393224 | tf_op jit(solution)/shard_map/ppermute | solution.py:209
  30.7 5.9 %collective-permute-start.7 = (f32[128,256]{1,0:T(8,128)S(1)}, f32[128,256]{1,0:T(8,128)S(1)}, u32[]{:S(2)}, u32[]{:S(2)}) collective-permute-start(f32[128,256]{1,0:T(8,128)S(1)} %get-tuple-element.51.refs_0_), channel_id=1, source_target_pairs={{0,8},{8,0},{16,24},{24,16},{1,9},{9,1},{17,25},{25,17},{2,10},{10... | collective-permute-start | bytes 393224 | tf_op jit(solution)/shard_map/ppermute | solution.py:209
  31.6 9.9 %collective-permute-start.14 = (f32[160,256]{1,0:T(8,128)S(1)}, f32[160,256]{1,0:T(8,128)S(1)}, u32[]{:S(2)}, u32[]{:S(2)}) collective-permute-start(f32[160,256]{1,0:T(8,128)S(1)} %get-tuple-element.57), channel_id=1, source_target_pairs={{0,1},{1,0},{2,3},{3,2},{4,5},{5,4},{6,7},{7,6},{8,9},{9,8},{10,11... | collective-permute-start | bytes 491528 | tf_op jit(solution)/shard_map/ppermute | solution.py:209
  37.0 6.4 %collective-permute-start.10 = (f32[64,256]{1,0:T(8,128)S(1)}, f32[64,256]{1,0:T(8,128)S(1)}, u32[]{:S(2)}, u32[]{:S(2)}) collective-permute-start(f32[64,256]{1,0:T(8,128)S(1)} %get-tuple-element.53), channel_id=1, source_target_pairs={{0,2},{1,3},{2,0},{3,1},{4,6},{5,7},{6,4},{7,5},{8,10},{9,11},{10,... | collective-permute-start | bytes 196616 | tf_op jit(solution)/shard_map/ppermute | solution.py:209
  37.1 9.1 %collective-permute-start.11 = (f32[64,256]{1,0:T(8,128)S(1)}, f32[64,256]{1,0:T(8,128)S(1)}, u32[]{:S(2)}, u32[]{:S(2)}) collective-permute-start(f32[64,256]{1,0:T(8,128)S(1)} %get-tuple-element.54), channel_id=1, source_target_pairs={{0,4},{1,5},{2,6},{3,7},{4,0},{5,1},{6,2},{7,3},{8,12},{9,13},{10,... | collective-permute-start | bytes 196616 | tf_op jit(solution)/shard_map/ppermute | solution.py:209
  39.5 13.6 %collective-permute-start.12 = (f32[64,256]{1,0:T(8,128)S(1)}, f32[64,256]{1,0:T(8,128)S(1)}, u32[]{:S(2)}, u32[]{:S(2)}) collective-permute-start(f32[64,256]{1,0:T(8,128)S(1)} %get-tuple-element.55), channel_id=1, source_target_pairs={{0,6},{1,7},{2,4},{3,5},{4,2},{5,3},{6,0},{7,1},{8,14},{9,15},{10,... | collective-permute-start | bytes 196616 | tf_op jit(solution)/shard_map/ppermute | solution.py:209
  41.5 6.0 %collective-permute-start.17 = (f32[40,256]{1,0:T(8,128)S(1)}, f32[40,256]{1,0:T(8,128)S(1)}, u32[]{:S(2)}, u32[]{:S(2)}) collective-permute-start(f32[40,256]{1,0:T(8,128)S(1)} %get-tuple-element.60), channel_id=1, source_target_pairs={{0,6},{1,7},{2,4},{3,5},{4,2},{5,3},{6,0},{7,1},{8,14},{9,15},{10,... | collective-permute-start | bytes 122888 | tf_op jit(solution)/shard_map/ppermute | solution.py:209
  43.4 6.1 %collective-permute-start.16 = (f32[40,256]{1,0:T(8,128)S(1)}, f32[40,256]{1,0:T(8,128)S(1)}, u32[]{:S(2)}, u32[]{:S(2)}) collective-permute-start(f32[40,256]{1,0:T(8,128)S(1)} %get-tuple-element.61), channel_id=1, source_target_pairs={{0,4},{1,5},{2,6},{3,7},{4,0},{5,1},{6,2},{7,3},{8,12},{9,13},{10,... | collective-permute-start | bytes 122888 | tf_op jit(solution)/shard_map/ppermute | solution.py:209
  43.4 6.1 %collective-permute-start.15 = (f32[40,256]{1,0:T(8,128)S(1)}, f32[40,256]{1,0:T(8,128)S(1)}, u32[]{:S(2)}, u32[]{:S(2)}) collective-permute-start(f32[40,256]{1,0:T(8,128)S(1)} %get-tuple-element.62), channel_id=1, source_target_pairs={{0,2},{1,3},{2,0},{3,1},{4,6},{5,7},{6,4},{7,5},{8,10},{9,11},{10,... | collective-permute-start | bytes 122888 | tf_op jit(solution)/shard_map/ppermute | solution.py:209
  49.6 5.4 %collective-permute-start.20 = (f32[40,256]{1,0:T(8,128)S(1)}, f32[40,256]{1,0:T(8,128)S(1)}, u32[]{:S(2)}, u32[]{:S(2)}) collective-permute-start(f32[40,256]{1,0:T(8,128)S(1)} %fusion), channel_id=1, source_target_pairs={{0,24},{8,16},{16,8},{24,0},{1,25},{9,17},{17,9},{25,1},{2,26},{10... | collective-permute-start | bytes 122888 | tf_op jit(solution)/shard_map/ppermute | solution.py:209
  51.4 4.0 %collective-permute-start.19 = (f32[40,256]{1,0:T(8,128)S(1)}, f32[40,256]{1,0:T(8,128)S(1)}, u32[]{:S(2)}, u32[]{:S(2)}) collective-permute-start(f32[40,256]{1,0:T(8,128)S(1)} %fusion), channel_id=1, source_target_pairs={{0,16},{8,24},{16,0},{24,8},{1,17},{9,25},{17,1},{25,9},{2,18},{10... | collective-permute-start | bytes 122888 | tf_op jit(solution)/shard_map/ppermute | solution.py:209
  52.9 4.0 %collective-permute-start.18 = (f32[40,256]{1,0:T(8,128)S(1)}, f32[40,256]{1,0:T(8,128)S(1)}, u32[]{:S(2)}, u32[]{:S(2)}) collective-permute-start(f32[40,256]{1,0:T(8,128)S(1)} %fusion), channel_id=1, source_target_pairs={{0,8},{8,0},{16,24},{24,16},{1,9},{9,1},{17,25},{25,17},{2,10},{10... | collective-permute-start | bytes 122888 | tf_op jit(solution)/shard_map/ppermute | solution.py:209
  56.9 5.8 %collective-permute-start.23 = (f32[32,256]{1,0:T(8,128)S(1)}, f32[32,256]{1,0:T(8,128)S(1)}, u32[]{:S(2)}, u32[]{:S(2)}) collective-permute-start(f32[32,256]{1,0:T(8,128)S(1)} %slice.100), channel_id=1, source_target_pairs={{0,6},{1,7},{2,4},{3,5},{4,2},{5,3},{6,0},{7,1},{8,14},{9,15},{10,... | collective-permute-start | bytes 98312 | tf_op jit(solution)/shard_map/ppermute | solution.py:209
  59.3 4.8 %collective-permute-start.22 = (f32[32,256]{1,0:T(8,128)S(1)}, f32[32,256]{1,0:T(8,128)S(1)}, u32[]{:S(2)}, u32[]{:S(2)}) collective-permute-start(f32[32,256]{1,0:T(8,128)S(1)} %slice.100), channel_id=1, source_target_pairs={{0,4},{1,5},{2,6},{3,7},{4,0},{5,1},{6,2},{7,3},{8,12},{9,13},{10,... | collective-permute-start | bytes 98312 | tf_op jit(solution)/shard_map/ppermute | solution.py:209
  59.3 4.8 %collective-permute-start.21 = (f32[32,256]{1,0:T(8,128)S(1)}, f32[32,256]{1,0:T(8,128)S(1)}, u32[]{:S(2)}, u32[]{:S(2)}) collective-permute-start(f32[32,256]{1,0:T(8,128)S(1)} %slice.100), channel_id=1, source_target_pairs={{0,2},{1,3},{2,0},{3,1},{4,6},{5,7},{6,4},{7,5},{8,10},{9,11},{10,... | collective-permute-start | bytes 98312 | tf_op jit(solution)/shard_map/ppermute | solution.py:209
  61.4 3.5 %collective-permute-start.13 = (f32[128,256]{1,0:T(8,128)S(1)}, f32[128,256]{1,0:T(8,128)S(1)}, u32[]{:S(2)}, u32[]{:S(2)}) collective-permute-start(f32[128,256]{1,0:T(8,128)S(1)} %pad_maximum_fusion.3), channel_id=1, source_target_pairs={{0,1},{1,0},{2,3},{3,2},{4,5},{5,4},{6,7},{7,6},{8,9},{9,8},{10,11... | collective-permute-start | bytes 393224 | tf_op jit(solution)/shard_map/ppermute | solution.py:209
  64.1 1.9 %collective-permute-start.24 = (f32[128,256]{1,0:T(8,128)S(1)}, f32[128,256]{1,0:T(8,128)S(1)}, u32[]{:S(2)}, u32[]{:S(2)}) collective-permute-start(f32[128,256]{1,0:T(8,128)S(1)} %pad_maximum_fusion.4.own_ref), channel_id=1, source_target_pairs={{0,1},{1,0},{2,3},{3,2},{4,5},{5,4},{6,7},{7,6},{8,9},{9,8},{10,11... | collective-permute-start | bytes 393224 | tf_op jit(solution)/shard_map/ppermute | solution.py:209

commit v3 on v2

--- a/solution.py
+++ b/solution.py
@@ -37,12 +37,19 @@
 
 
 def mm3(a, b, dims):
-    return mm(a[0], b[0], dims) + (mm(a[0], b[1], dims) + mm(a[1], b[0], dims))
-
-
-def mm6(a, b, dims):
-    small = mm(a[0], b[2], dims) + mm(a[1], b[1], dims) + mm(a[2], b[0], dims)
-    return mm(a[0], b[0], dims) + (mm(a[0], b[1], dims) + mm(a[1], b[0], dims) + small)
+    if dims == TN:
+        return mm(a[0], b[0], dims) + (mm(a[0], b[1], dims) + mm(a[1], b[0], dims))
+    rows = a[0].shape[0]
+    first = mm(jnp.concatenate(a[:2], axis=0), b[0], dims)
+    return first[:rows] + (mm(a[0], b[1], dims) + first[rows:])
+
+
+def mm6(a, b):
+    rows = a[0].shape[0]
+    first = mm(jnp.concatenate(a, axis=0), b[0], NN)
+    second = mm(jnp.concatenate(a[:2], axis=0), b[1], NN)
+    small = mm(a[0], b[2], NN) + second[rows:] + first[2 * rows :]
+    return first[:rows] + (second[:rows] + first[rows : 2 * rows] + small)
 
 
 def selected(pick, x):
@@ -140,7 +147,7 @@
             pieces.append(half[pair * per : (pair + 1) * per, :])
     border = jnp.concatenate(pieces, axis=0)
     dense = high_ref[...], middle_ref[...], low_ref[...]
-    result = mm6(dense, split3(border), NN)
+    result = mm6(dense, split3(border))
     for s, out in enumerate(outs):
         out[...] = result[s * out.shape[0] : (s + 1) * out.shape[0], :]
 
@@ -152,7 +159,7 @@
     total = tree_sum([piece[...] for piece in pieces])
     total_split = split3(total)
     weight = high_ref[...], middle_ref[...], low_ref[...]
-    pre = mm6(total_split, weight, NN) + bias_ref[...]
+    pre = mm6(total_split, weight) + bias_ref[...]
     gate = jax.nn.sigmoid(pre)
     pre_ref[...] = pre
     grad = cot_ref[...] * (gate * (1.0 + pre * (1.0 - gate)))

time: 67 us -> 67 us (level)
  no operation moved by 1% of the time
where the time goes in v3:
time: 67 us; the launch traced here: 66.7 us
  starting transfers between devices  29.9 us (45%)
  waiting for transfers between devices  27 us (40%)
  Pallas kernels  7.91 us (12%)
  between operations  1.48 us (2%)
    ppermute x25, starting transfers between devices, exchange(): return lax.ppermute(value, axis, [(i, i ^ shift) for i in range(size)])  29.9 us
    ppermute x25, waiting for transfers between devices, exchange(): return lax.ppermute(value, axis, [(i, i ^ shift) for i in range(size)])  27 us
    pallas_call x9, Pallas kernels, call(): pl.pallas_call(kernel, out_shape=outs, in_specs=[pl.BlockSpec(memory_spac...  7.91 us
  transfers between devices with their start and end apart: 25, of which 15 were waited for; matrix products, arithmetic and copies ran while one was open for 0% of the time, Pallas kernels for 7%

profile of v3, /device:TPU:0, one launch (start us, length us, event | category | flops | bytes accessed | tf_op | source)
XLA Modules:
  0.0 66.7 jit_solution(177191131941674269)
XLA Ops:
  0.6 1.2 %shard_map.121 = (f32[64,256]{1,0:T(8,128)S(1)}, f32[64,256]{1,0:T(8,128)S(1)}, f32[64,256]{1,0:T(8,128)S(1)}, f32[64,256]{1,0:T(8,128)S(1)}, s32[1,256]{1,0:T(1,128)S(1)}) custom-call(s32[1,2048]{1,0:T(1,128)} %list_hbm.1, f32[128,256]{1,0:T(8,128)} %feat_hbm.1), custom_call_target="tpu_custom_call" | custom-call | bytes 402432 | tf_op jit(solution)/shard_map/pallas_call | solution.py:64
  1.8 3.1 %collective-permute-start = (f32[64,256]{1,0:T(8,128)S(1)}, f32[64,256]{1,0:T(8,128)S(1)}, u32[]{:S(2)}, u32[]{:S(2)}) collective-permute-start(f32[64,256]{1,0:T(8,128)S(1)} %get-tuple-element.36), channel_id=1, source_target_pairs={{0,2},{1,3},{2,0},{3,1},{4,6},{5,7},{6,4},{7,5},{8,10},{9,11},{10,... | collective-permute-start | bytes 196616 | tf_op jit(solution)/shard_map/ppermute | solution.py:216
  4.9 2.6 %collective-permute-start.1 = (f32[64,256]{1,0:T(8,128)S(1)}, f32[64,256]{1,0:T(8,128)S(1)}, u32[]{:S(2)}, u32[]{:S(2)}) collective-permute-start(f32[64,256]{1,0:T(8,128)S(1)} %get-tuple-element.37), channel_id=1, source_target_pairs={{0,4},{1,5},{2,6},{3,7},{4,0},{5,1},{6,2},{7,3},{8,12},{9,13},{10,... | collective-permute-start | bytes 196616 | tf_op jit(solution)/shard_map/ppermute | solution.py:216
  7.5 0.0 collective-permute-start.2
  7.5 0.0 collective-permute-done
  7.5 4.6 %collective-permute-done.1 = f32[64,256]{1,0:T(8,128)S(1)} collective-permute-done((f32[64,256]{1,0:T(8,128)S(1)}, f32[64,256]{1,0:T(8,128)S(1)}, u32[]{:S(2)}, u32[]{:S(2)}) %collective-permute-start.1) | collective-permute-done | bytes 65568 | tf_op jit(solution)/shard_map/ppermute | solution.py:216
  12.2 1.4 %collective-permute-done.2 = f32[64,256]{1,0:T(8,128)S(1)} collective-permute-done((f32[64,256]{1,0:T(8,128)S(1)}, f32[64,256]{1,0:T(8,128)S(1)}, u32[]{:S(2)}, u32[]{:S(2)}) %collective-permute-start.2) | collective-permute-done | bytes 65568 | tf_op jit(solution)/shard_map/ppermute | solution.py:216
  13.6 0.1 collective-permute-start.3
  14.3 2.3 %shard_map.120 = (bf16[512,256]{1,0:T(8,128)(2,1)S(1)}, bf16[512,256]{1,0:T(8,128)(2,1)S(1)}, bf16[512,256]{1,0:T(8,128)(2,1)S(1)}) custom-call(s32[1,1]{1,0:T(1,128)S(6)} %copy.13.live_ref, s32[1,64]{1,0:T(1,128)} %bitcast.7, s32[1,64]{1,0:T(1,128)} %bitcast.8, f32[64,4096]{1,0:T(8,128)} %bitcast.6), custom_call_target="tpu_custom_call" | custom-call | flops 33554432 | bytes 1835524 | tf_op jit(solution)/shard_map/pallas_call | solution.py:64
  16.6 0.0 collective-permute-done.3.partner_ref
  16.7 0.0 copy-start
  16.7 0.6 shard_map.122
  17.3 1.6 %collective-permute-start.4 = (f32[128,256]{1,0:T(8,128)S(1)}, f32[128,256]{1,0:T(8,128)S(1)}, u32[]{:S(2)}, u32[]{:S(2)}) collective-permute-start(f32[128,256]{1,0:T(8,128)S(1)} %get-tuple-element.40), channel_id=1, source_target_pairs={{0,8},{8,0},{16,24},{24,16},{1,9},{9,1},{17,25},{25,17},{2,10},{10... | collective-permute-start | bytes 393224 | tf_op jit(solution)/shard_map/ppermute | solution.py:216
  18.8 1.5 %collective-permute-start.5 = (f32[128,256]{1,0:T(8,128)S(1)}, f32[128,256]{1,0:T(8,128)S(1)}, u32[]{:S(2)}, u32[]{:S(2)}) collective-permute-start(f32[128,256]{1,0:T(8,128)S(1)} %get-tuple-element.41), channel_id=1, source_target_pairs={{0,16},{8,24},{16,0},{24,8},{1,17},{9,25},{17,1},{25,9},{2,18},{10... | collective-permute-start | bytes 393224 | tf_op jit(solution)/shard_map/ppermute | solution.py:216
  20.4 0.5 collective-permute-start.6
  20.8 0.0 copy-done
  20.8 0.2 copy-done.2
  21.0 0.0 copy-start.1
  21.0 0.3 shard_map.123
  21.3 2.4 %collective-permute-done.4.refs_1_ = f32[128,256]{1,0:T(8,128)S(1)} collective-permute-done((f32[128,256]{1,0:T(8,128)S(1)}, f32[128,256]{1,0:T(8,128)S(1)}, u32[]{:S(2)}, u32[]{:S(2)}) %collective-permute-start.4) | collective-permute-done | bytes 131104 | tf_op jit(solution)/shard_map/ppermute | solution.py:216
  23.6 3.6 %collective-permute-done.5.refs_2_ = f32[128,256]{1,0:T(8,128)S(1)} collective-permute-done((f32[128,256]{1,0:T(8,128)S(1)}, f32[128,256]{1,0:T(8,128)S(1)}, u32[]{:S(2)}, u32[]{:S(2)}) %collective-permute-start.5) | collective-permute-done | bytes 131104 | tf_op jit(solution)/shard_map/ppermute | solution.py:216
  27.3 0.0 collective-permute-done.6.refs_3_
  27.3 0.0 copy-done.1
  27.3 0.7 %shard_map.124 = (f32[128,256]{1,0:T(8,128)S(1)}, f32[128,256]{1,0:T(8,128)S(1)}, f32[160,256]{1,0:T(8,128)S(1)}, f32[160,256]{1,0:T(8,128)S(1)}) custom-call(f32[128,256]{1,0:T(8,128)S(1)} %get-tuple-element.39.refs_0_, f32[128,256]{1,0:T(8,128)S(1)} %collective-permute-done.4.refs_1_, f32[128,256]{1,0:T(8,128)S(1)} %collective-permute-done.5.refs_2_, ...), custom_call_target="tpu_custom_call" | custom-call | flops 100663296 | bytes 1639424 | tf_op jit(solution)/shard_map/pallas_call | solution.py:64
  28.0 1.6 %collective-permute-start.9 = (f32[128,256]{1,0:T(8,128)S(1)}, f32[128,256]{1,0:T(8,128)S(1)}, u32[]{:S(2)}, u32[]{:S(2)}) collective-permute-start(f32[128,256]{1,0:T(8,128)S(1)} %get-tuple-element.51.refs_0_), channel_id=1, source_target_pairs={{0,24},{8,16},{16,8},{24,0},{1,25},{9,17},{17,9},{25,1},{2,26},{10... | collective-permute-start | bytes 393224 | tf_op jit(solution)/shard_map/ppermute | solution.py:216
  29.6 1.2 %collective-permute-start.8 = (f32[128,256]{1,0:T(8,128)S(1)}, f32[128,256]{1,0:T(8,128)S(1)}, u32[]{:S(2)}, u32[]{:S(2)}) collective-permute-start(f32[128,256]{1,0:T(8,128)S(1)} %get-tuple-element.51.refs_0_), channel_id=1, source_target_pairs={{0,16},{8,24},{16,0},{24,8},{1,17},{9,25},{17,1},{25,9},{2,18},{10... | collective-permute-start | bytes 393224 | tf_op jit(solution)/shard_map/ppermute | solution.py:216
  30.7 0.8 %collective-permute-start.7 = (f32[128,256]{1,0:T(8,128)S(1)}, f32[128,256]{1,0:T(8,128)S(1)}, u32[]{:S(2)}, u32[]{:S(2)}) collective-permute-start(f32[128,256]{1,0:T(8,128)S(1)} %get-tuple-element.51.refs_0_), channel_id=1, source_target_pairs={{0,8},{8,0},{16,24},{24,16},{1,9},{9,1},{17,25},{25,17},{2,10},{10... | collective-permute-start | bytes 393224 | tf_op jit(solution)/shard_map/ppermute | solution.py:216
  31.6 0.0 collective-permute-start.14
  31.6 3.7 %collective-permute-done.9.refs_3_ = f32[128,256]{1,0:T(8,128)S(1)} collective-permute-done((f32[128,256]{1,0:T(8,128)S(1)}, f32[128,256]{1,0:T(8,128)S(1)}, u32[]{:S(2)}, u32[]{:S(2)}) %collective-permute-start.9) | collective-permute-done | bytes 131104 | tf_op jit(solution)/shard_map/ppermute | solution.py:216
  35.2 1.2 %collective-permute-done.8.refs_2_ = f32[128,256]{1,0:T(8,128)S(1)} collective-permute-done((f32[128,256]{1,0:T(8,128)S(1)}, f32[128,256]{1,0:T(8,128)S(1)}, u32[]{:S(2)}, u32[]{:S(2)}) %collective-permute-start.8) | collective-permute-done | bytes 131104 | tf_op jit(solution)/shard_map/ppermute | solution.py:216
  36.5 0.2 collective-permute-done.7.refs_1_
  36.6 0.4 shard_map.126
  37.0 0.1 collective-permute-start.10
  37.1 2.4 %collective-permute-start.11 = (f32[64,256]{1,0:T(8,128)S(1)}, f32[64,256]{1,0:T(8,128)S(1)}, u32[]{:S(2)}, u32[]{:S(2)}) collective-permute-start(f32[64,256]{1,0:T(8,128)S(1)} %get-tuple-element.54), channel_id=1, source_target_pairs={{0,4},{1,5},{2,6},{3,7},{4,0},{5,1},{6,2},{7,3},{8,12},{9,13},{10,... | collective-permute-start | bytes 196616 | tf_op jit(solution)/shard_map/ppermute | solution.py:216
  39.5 2.0 %collective-permute-start.12 = (f32[64,256]{1,0:T(8,128)S(1)}, f32[64,256]{1,0:T(8,128)S(1)}, u32[]{:S(2)}, u32[]{:S(2)}) collective-permute-start(f32[64,256]{1,0:T(8,128)S(1)} %get-tuple-element.55), channel_id=1, source_target_pairs={{0,6},{1,7},{2,4},{3,5},{4,2},{5,3},{6,0},{7,1},{8,14},{9,15},{10,... | collective-permute-start | bytes 196616 | tf_op jit(solution)/shard_map/ppermute | solution.py:216
  41.5 0.0 collective-permute-done.14
  41.5 1.9 %collective-permute-start.17 = (f32[40,256]{1,0:T(8,128)S(1)}, f32[40,256]{1,0:T(8,128)S(1)}, u32[]{:S(2)}, u32[]{:S(2)}) collective-permute-start(f32[40,256]{1,0:T(8,128)S(1)} %get-tuple-element.60), channel_id=1, source_target_pairs={{0,6},{1,7},{2,4},{3,5},{4,2},{5,3},{6,0},{7,1},{8,14},{9,15},{10,... | collective-permute-start | bytes 122888 | tf_op jit(solution)/shard_map/ppermute | solution.py:216
  43.4 0.0 collective-permute-start.16
  43.4 0.0 collective-permute-done.10
  43.4 2.6 %collective-permute-start.15 = (f32[40,256]{1,0:T(8,128)S(1)}, f32[40,256]{1,0:T(8,128)S(1)}, u32[]{:S(2)}, u32[]{:S(2)}) collective-permute-start(f32[40,256]{1,0:T(8,128)S(1)} %get-tuple-element.62), channel_id=1, source_target_pairs={{0,2},{1,3},{2,0},{3,1},{4,6},{5,7},{6,4},{7,5},{8,10},{9,11},{10,... | collective-permute-start | bytes 122888 | tf_op jit(solution)/shard_map/ppermute | solution.py:216
  46.0 0.2 collective-permute-done.11
  46.2 1.3 %collective-permute-done.17 = f32[40,256]{1,0:T(8,128)S(1)} collective-permute-done((f32[40,256]{1,0:T(8,128)S(1)}, f32[40,256]{1,0:T(8,128)S(1)}, u32[]{:S(2)}, u32[]{:S(2)}) %collective-permute-start.17) | collective-permute-done | bytes 40992 | tf_op jit(solution)/shard_map/ppermute | solution.py:216
  47.5 2.1 %collective-permute-done.16 = f32[40,256]{1,0:T(8,128)S(1)} collective-permute-done((f32[40,256]{1,0:T(8,128)S(1)}, f32[40,256]{1,0:T(8,128)S(1)}, u32[]{:S(2)}, u32[]{:S(2)}) %collective-permute-start.16) | collective-permute-done | bytes 40992 | tf_op jit(solution)/shard_map/ppermute | solution.py:216
  49.6 0.0 collective-permute-done.15
  49.6 1.8 %collective-permute-start.20 = (f32[40,256]{1,0:T(8,128)S(1)}, f32[40,256]{1,0:T(8,128)S(1)}, u32[]{:S(2)}, u32[]{:S(2)}) collective-permute-start(f32[40,256]{1,0:T(8,128)S(1)} %fusion), channel_id=1, source_target_pairs={{0,24},{8,16},{16,8},{24,0},{1,25},{9,17},{17,9},{25,1},{2,26},{10... | collective-permute-start | bytes 122888 | tf_op jit(solution)/shard_map/ppermute | solution.py:216
  51.4 1.5 %collective-permute-start.19 = (f32[40,256]{1,0:T(8,128)S(1)}, f32[40,256]{1,0:T(8,128)S(1)}, u32[]{:S(2)}, u32[]{:S(2)}) collective-permute-start(f32[40,256]{1,0:T(8,128)S(1)} %fusion), channel_id=1, source_target_pairs={{0,16},{8,24},{16,0},{24,8},{1,17},{9,25},{17,1},{25,9},{2,18},{10... | collective-permute-start | bytes 122888 | tf_op jit(solution)/shard_map/ppermute | solution.py:216
  52.9 0.2 collective-permute-start.18
  53.1 0.0 collective-permute-done.12
  53.1 1.8 %collective-permute-done.20 = f32[40,256]{1,0:T(8,128)S(1)} collective-permute-done((f32[40,256]{1,0:T(8,128)S(1)}, f32[40,256]{1,0:T(8,128)S(1)}, u32[]{:S(2)}, u32[]{:S(2)}) %collective-permute-start.20) | collective-permute-done | bytes 40992 | tf_op jit(solution)/shard_map/ppermute | solution.py:216
  54.9 0.4 collective-permute-done.19
  55.4 1.5 %collective-permute-done.18 = f32[40,256]{1,0:T(8,128)S(1)} collective-permute-done((f32[40,256]{1,0:T(8,128)S(1)}, f32[40,256]{1,0:T(8,128)S(1)}, u32[]{:S(2)}, u32[]{:S(2)}) %collective-permute-start.18) | collective-permute-done | bytes 40992 | tf_op jit(solution)/shard_map/ppermute | solution.py:216
  56.9 2.4 %collective-permute-start.23 = (f32[32,256]{1,0:T(8,128)S(1)}, f32[32,256]{1,0:T(8,128)S(1)}, u32[]{:S(2)}, u32[]{:S(2)}) collective-permute-start(f32[32,256]{1,0:T(8,128)S(1)} %slice.100), channel_id=1, source_target_pairs={{0,6},{1,7},{2,4},{3,5},{4,2},{5,3},{6,0},{7,1},{8,14},{9,15},{10,... | collective-permute-start | bytes 98312 | tf_op jit(solution)/shard_map/ppermute | solution.py:216
  59.3 0.0 collective-permute-start.22
  59.3 2.1 %collective-permute-start.21 = (f32[32,256]{1,0:T(8,128)S(1)}, f32[32,256]{1,0:T(8,128)S(1)}, u32[]{:S(2)}, u32[]{:S(2)}) collective-permute-start(f32[32,256]{1,0:T(8,128)S(1)} %slice.100), channel_id=1, source_target_pairs={{0,2},{1,3},{2,0},{3,1},{4,6},{5,7},{6,4},{7,5},{8,10},{9,11},{10,... | collective-permute-start | bytes 98312 | tf_op jit(solution)/shard_map/ppermute | solution.py:216
  61.4 0.1 collective-permute-start.13
  61.5 1.2 %collective-permute-done.23 = f32[32,256]{1,0:T(8,128)S(1)} collective-permute-done((f32[32,256]{1,0:T(8,128)S(1)}, f32[32,256]{1,0:T(8,128)S(1)}, u32[]{:S(2)}, u32[]{:S(2)}) %collective-permute-start.23) | collective-permute-done | bytes 32800 | tf_op jit(solution)/shard_map/ppermute | solution.py:216
  62.7 1.4 %collective-permute-done.22 = f32[32,256]{1,0:T(8,128)S(1)} collective-permute-done((f32[32,256]{1,0:T(8,128)S(1)}, f32[32,256]{1,0:T(8,128)S(1)}, u32[]{:S(2)}, u32[]{:S(2)}) %collective-permute-start.22) | collective-permute-done | bytes 32800 | tf_op jit(solution)/shard_map/ppermute | solution.py:216
  64.1 0.0 collective-permute-done.21
  64.1 0.1 collective-permute-start.24
  64.2 0.7 %shard_map.125 = f32[128,256]{1,0:T(8,128)} custom-call(f32[128,256]{1,0:T(8,128)S(1)} %get-tuple-element.47.pre_ref), custom_call_target="tpu_custom_call" | custom-call | bytes 262144 | tf_op jit(solution)/shard_map/pallas_call | solution.py:64
  64.9 0.0 collective-permute-done.13.partner_ref
  64.9 1.1 %shard_map.127 = f32[128,256]{1,0:T(8,128)} custom-call(s32[1,256]{1,0:T(1,128)S(1)} %get-tuple-element.48.wanted_ref, bf16[256,256]{1,0:T(8,128)(2,1)S(1)} %get-tuple-element.43.refs_4_.high_ref, bf16[256,256]{1,0:T(8,128)(2,1)S(1)} %get-tuple-element.44.refs_5_.low_ref, f32[128,256]{1,0:T(8,128)S(1)} %pad_maximum_fusion.2.own_ref, ...), custom_call_target="tpu_custom_call" | custom-call | flops 50331648 | bytes 656384 | tf_op jit(solution)/shard_map/pallas_call | solution.py:64
  66.0 0.0 collective-permute-done.24.partner_ref
  66.0 0.7 %shard_map.128 = (f32[256,256]{1,0:T(8,128)}, f32[1,256]{1,0:T(1,128)}) custom-call(f32[40,256]{1,0:T(8,128)S(1)} %add_add_fusion.summed_ref, f32[128,256]{1,0:T(8,128)S(1)} %pad_maximum_fusion.4.own_ref, f32[128,256]{1,0:T(8,128)S(1)} %collective-permute-done.24.partner_ref), custom_call_target="tpu_custom_call" | custom-call | bytes 566272 | tf_op jit(solution)/shard_map/pallas_call | solution.py:64
  (19 shorter events, 0.2 us)
Async XLA Ops:
  1.8 5.7 %collective-permute-start = (f32[64,256]{1,0:T(8,128)S(1)}, f32[64,256]{1,0:T(8,128)S(1)}, u32[]{:S(2)}, u32[]{:S(2)}) collective-permute-start(f32[64,256]{1,0:T(8,128)S(1)} %get-tuple-element.36), channel_id=1, source_target_pairs={{0,2},{1,3},{2,0},{3,1},{4,6},{5,7},{6,4},{7,5},{8,10},{9,11},{10,... | collective-permute-start | bytes 196616 | tf_op jit(solution)/shard_map/ppermute | solution.py:216
  4.9 7.3 %collective-permute-start.1 = (f32[64,256]{1,0:T(8,128)S(1)}, f32[64,256]{1,0:T(8,128)S(1)}, u32[]{:S(2)}, u32[]{:S(2)}) collective-permute-start(f32[64,256]{1,0:T(8,128)S(1)} %get-tuple-element.37), channel_id=1, source_target_pairs={{0,4},{1,5},{2,6},{3,7},{4,0},{5,1},{6,2},{7,3},{8,12},{9,13},{10,... | collective-permute-start | bytes 196616 | tf_op jit(solution)/shard_map/ppermute | solution.py:216
  7.5 6.1 %collective-permute-start.2 = (f32[64,256]{1,0:T(8,128)S(1)}, f32[64,256]{1,0:T(8,128)S(1)}, u32[]{:S(2)}, u32[]{:S(2)}) collective-permute-start(f32[64,256]{1,0:T(8,128)S(1)} %get-tuple-element.38), channel_id=1, source_target_pairs={{0,6},{1,7},{2,4},{3,5},{4,2},{5,3},{6,0},{7,1},{8,14},{9,15},{10,... | collective-permute-start | bytes 196616 | tf_op jit(solution)/shard_map/ppermute | solution.py:216
  13.6 3.1 %collective-permute-start.3 = (f32[128,256]{1,0:T(8,128)S(1)}, f32[128,256]{1,0:T(8,128)S(1)}, u32[]{:S(2)}, u32[]{:S(2)}) collective-permute-start(f32[128,256]{1,0:T(8,128)S(1)} %pad_maximum_fusion.1), channel_id=1, source_target_pairs={{0,1},{1,0},{2,3},{3,2},{4,5},{5,4},{6,7},{7,6},{8,9},{9,8},{10,11... | collective-permute-start | bytes 393224 | tf_op jit(solution)/shard_map/ppermute | solution.py:216
  16.7 4.2 %copy-start = (f32[256,256]{1,0:T(8,128)S(1)}, f32[256,256]{1,0:T(8,128)}, u32[]{:S(2)}) copy-start(f32[256,256]{1,0:T(8,128)} %weight_ref.1) | copy-start | bytes 786436
  17.3 6.4 %collective-permute-start.4 = (f32[128,256]{1,0:T(8,128)S(1)}, f32[128,256]{1,0:T(8,128)S(1)}, u32[]{:S(2)}, u32[]{:S(2)}) collective-permute-start(f32[128,256]{1,0:T(8,128)S(1)} %get-tuple-element.40), channel_id=1, source_target_pairs={{0,8},{8,0},{16,24},{24,16},{1,9},{9,1},{17,25},{25,17},{2,10},{10... | collective-permute-start | bytes 393224 | tf_op jit(solution)/shard_map/ppermute | solution.py:216
  18.8 8.4 %collective-permute-start.5 = (f32[128,256]{1,0:T(8,128)S(1)}, f32[128,256]{1,0:T(8,128)S(1)}, u32[]{:S(2)}, u32[]{:S(2)}) collective-permute-start(f32[128,256]{1,0:T(8,128)S(1)} %get-tuple-element.41), channel_id=1, source_target_pairs={{0,16},{8,24},{16,0},{24,8},{1,17},{9,25},{17,1},{25,9},{2,18},{10... | collective-permute-start | bytes 393224 | tf_op jit(solution)/shard_map/ppermute | solution.py:216
  20.3 0.7 %copy-start.2 = (f32[256]{0:T(256)S(1)}, f32[256]{0:T(256)}, u32[]{:S(2)}) copy-start(f32[256]{0:T(256)} %param.11) | copy-start | bytes 3076
  20.4 6.9 %collective-permute-start.6 = (f32[128,256]{1,0:T(8,128)S(1)}, f32[128,256]{1,0:T(8,128)S(1)}, u32[]{:S(2)}, u32[]{:S(2)}) collective-permute-start(f32[128,256]{1,0:T(8,128)S(1)} %get-tuple-element.42), channel_id=1, source_target_pairs={{0,24},{8,16},{16,8},{24,0},{1,25},{9,17},{17,9},{25,1},{2,26},{10... | collective-permute-start | bytes 393224 | tf_op jit(solution)/shard_map/ppermute | solution.py:216
  21.0 6.2 %copy-start.1 = (f32[128,256]{1,0:T(8,128)S(1)}, f32[128,256]{1,0:T(8,128)}, u32[]{:S(2)}) copy-start(f32[128,256]{1,0:T(8,128)} %refs_8_.1) | copy-start | bytes 393220
  28.0 7.2 %collective-permute-start.9 = (f32[128,256]{1,0:T(8,128)S(1)}, f32[128,256]{1,0:T(8,128)S(1)}, u32[]{:S(2)}, u32[]{:S(2)}) collective-permute-start(f32[128,256]{1,0:T(8,128)S(1)} %get-tuple-element.51.refs_0_), channel_id=1, source_target_pairs={{0,24},{8,16},{16,8},{24,0},{1,25},{9,17},{17,9},{25,1},{2,26},{10... | collective-permute-start | bytes 393224 | tf_op jit(solution)/shard_map/ppermute | solution.py:216
  29.6 6.9 %collective-permute-start.8 = (f32[128,256]{1,0:T(8,128)S(1)}, f32[128,256]{1,0:T(8,128)S(1)}, u32[]{:S(2)}, u32[]{:S(2)}) collective-permute-start(f32[128,256]{1,0:T(8,128)S(1)} %get-tuple-element.51.refs_0_), channel_id=1, source_target_pairs={{0,16},{8,24},{16,0},{24,8},{1,17},{9,25},{17,1},{25,9},{2,18},{10... | collective-permute-start | bytes 393224 | tf_op jit(solution)/shard_map/ppermute | solution.py:216
  30.7 5.9 %collective-permute-start.7 = (f32[128,256]{1,0:T(8,128)S(1)}, f32[128,256]{1,0:T(8,128)S(1)}, u32[]{:S(2)}, u32[]{:S(2)}) collective-permute-start(f32[128,256]{1,0:T(8,128)S(1)} %get-tuple-element.51.refs_0_), channel_id=1, source_target_pairs={{0,8},{8,0},{16,24},{24,16},{1,9},{9,1},{17,25},{25,17},{2,10},{10... | collective-permute-start | bytes 393224 | tf_op jit(solution)/shard_map/ppermute | solution.py:216
  31.6 9.9 %collective-permute-start.14 = (f32[160,256]{1,0:T(8,128)S(1)}, f32[160,256]{1,0:T(8,128)S(1)}, u32[]{:S(2)}, u32[]{:S(2)}) collective-permute-start(f32[160,256]{1,0:T(8,128)S(1)} %get-tuple-element.57), channel_id=1, source_target_pairs={{0,1},{1,0},{2,3},{3,2},{4,5},{5,4},{6,7},{7,6},{8,9},{9,8},{10,11... | collective-permute-start | bytes 491528 | tf_op jit(solution)/shard_map/ppermute | solution.py:216
  37.0 6.4 %collective-permute-start.10 = (f32[64,256]{1,0:T(8,128)S(1)}, f32[64,256]{1,0:T(8,128)S(1)}, u32[]{:S(2)}, u32[]{:S(2)}) collective-permute-start(f32[64,256]{1,0:T(8,128)S(1)} %get-tuple-element.53), channel_id=1, source_target_pairs={{0,2},{1,3},{2,0},{3,1},{4,6},{5,7},{6,4},{7,5},{8,10},{9,11},{10,... | collective-permute-start | bytes 196616 | tf_op jit(solution)/shard_map/ppermute | solution.py:216
  37.1 9.1 %collective-permute-start.11 = (f32[64,256]{1,0:T(8,128)S(1)}, f32[64,256]{1,0:T(8,128)S(1)}, u32[]{:S(2)}, u32[]{:S(2)}) collective-permute-start(f32[64,256]{1,0:T(8,128)S(1)} %get-tuple-element.54), channel_id=1, source_target_pairs={{0,4},{1,5},{2,6},{3,7},{4,0},{5,1},{6,2},{7,3},{8,12},{9,13},{10,... | collective-permute-start | bytes 196616 | tf_op jit(solution)/shard_map/ppermute | solution.py:216
  39.5 13.7 %collective-permute-start.12 = (f32[64,256]{1,0:T(8,128)S(1)}, f32[64,256]{1,0:T(8,128)S(1)}, u32[]{:S(2)}, u32[]{:S(2)}) collective-permute-start(f32[64,256]{1,0:T(8,128)S(1)} %get-tuple-element.55), channel_id=1, source_target_pairs={{0,6},{1,7},{2,4},{3,5},{4,2},{5,3},{6,0},{7,1},{8,14},{9,15},{10,... | collective-permute-start | bytes 196616 | tf_op jit(solution)/shard_map/ppermute | solution.py:216
  41.5 6.0 %collective-permute-start.17 = (f32[40,256]{1,0:T(8,128)S(1)}, f32[40,256]{1,0:T(8,128)S(1)}, u32[]{:S(2)}, u32[]{:S(2)}) collective-permute-start(f32[40,256]{1,0:T(8,128)S(1)} %get-tuple-element.60), channel_id=1, source_target_pairs={{0,6},{1,7},{2,4},{3,5},{4,2},{5,3},{6,0},{7,1},{8,14},{9,15},{10,... | collective-permute-start | bytes 122888 | tf_op jit(solution)/shard_map/ppermute | solution.py:216
  43.4 6.1 %collective-permute-start.16 = (f32[40,256]{1,0:T(8,128)S(1)}, f32[40,256]{1,0:T(8,128)S(1)}, u32[]{:S(2)}, u32[]{:S(2)}) collective-permute-start(f32[40,256]{1,0:T(8,128)S(1)} %get-tuple-element.61), channel_id=1, source_target_pairs={{0,4},{1,5},{2,6},{3,7},{4,0},{5,1},{6,2},{7,3},{8,12},{9,13},{10,... | collective-permute-start | bytes 122888 | tf_op jit(solution)/shard_map/ppermute | solution.py:216
  43.4 6.1 %collective-permute-start.15 = (f32[40,256]{1,0:T(8,128)S(1)}, f32[40,256]{1,0:T(8,128)S(1)}, u32[]{:S(2)}, u32[]{:S(2)}) collective-permute-start(f32[40,256]{1,0:T(8,128)S(1)} %get-tuple-element.62), channel_id=1, source_target_pairs={{0,2},{1,3},{2,0},{3,1},{4,6},{5,7},{6,4},{7,5},{8,10},{9,11},{10,... | collective-permute-start | bytes 122888 | tf_op jit(solution)/shard_map/ppermute | solution.py:216
  49.6 5.3 %collective-permute-start.20 = (f32[40,256]{1,0:T(8,128)S(1)}, f32[40,256]{1,0:T(8,128)S(1)}, u32[]{:S(2)}, u32[]{:S(2)}) collective-permute-start(f32[40,256]{1,0:T(8,128)S(1)} %fusion), channel_id=1, source_target_pairs={{0,24},{8,16},{16,8},{24,0},{1,25},{9,17},{17,9},{25,1},{2,26},{10... | collective-permute-start | bytes 122888 | tf_op jit(solution)/shard_map/ppermute | solution.py:216
  51.4 4.0 %collective-permute-start.19 = (f32[40,256]{1,0:T(8,128)S(1)}, f32[40,256]{1,0:T(8,128)S(1)}, u32[]{:S(2)}, u32[]{:S(2)}) collective-permute-start(f32[40,256]{1,0:T(8,128)S(1)} %fusion), channel_id=1, source_target_pairs={{0,16},{8,24},{16,0},{24,8},{1,17},{9,25},{17,1},{25,9},{2,18},{10... | collective-permute-start | bytes 122888 | tf_op jit(solution)/shard_map/ppermute | solution.py:216
  52.9 4.0 %collective-permute-start.18 = (f32[40,256]{1,0:T(8,128)S(1)}, f32[40,256]{1,0:T(8,128)S(1)}, u32[]{:S(2)}, u32[]{:S(2)}) collective-permute-start(f32[40,256]{1,0:T(8,128)S(1)} %fusion), channel_id=1, source_target_pairs={{0,8},{8,0},{16,24},{24,16},{1,9},{9,1},{17,25},{25,17},{2,10},{10... | collective-permute-start | bytes 122888 | tf_op jit(solution)/shard_map/ppermute | solution.py:216
  56.9 5.8 %collective-permute-start.23 = (f32[32,256]{1,0:T(8,128)S(1)}, f32[32,256]{1,0:T(8,128)S(1)}, u32[]{:S(2)}, u32[]{:S(2)}) collective-permute-start(f32[32,256]{1,0:T(8,128)S(1)} %slice.100), channel_id=1, source_target_pairs={{0,6},{1,7},{2,4},{3,5},{4,2},{5,3},{6,0},{7,1},{8,14},{9,15},{10,... | collective-permute-start | bytes 98312 | tf_op jit(solution)/shard_map/ppermute | solution.py:216
  59.3 4.8 %collective-permute-start.22 = (f32[32,256]{1,0:T(8,128)S(1)}, f32[32,256]{1,0:T(8,128)S(1)}, u32[]{:S(2)}, u32[]{:S(2)}) collective-permute-start(f32[32,256]{1,0:T(8,128)S(1)} %slice.100), channel_id=1, source_target_pairs={{0,4},{1,5},{2,6},{3,7},{4,0},{5,1},{6,2},{7,3},{8,12},{9,13},{10,... | collective-permute-start | bytes 98312 | tf_op jit(solution)/shard_map/ppermute | solution.py:216
  59.3 4.8 %collective-permute-start.21 = (f32[32,256]{1,0:T(8,128)S(1)}, f32[32,256]{1,0:T(8,128)S(1)}, u32[]{:S(2)}, u32[]{:S(2)}) collective-permute-start(f32[32,256]{1,0:T(8,128)S(1)} %slice.100), channel_id=1, source_target_pairs={{0,2},{1,3},{2,0},{3,1},{4,6},{5,7},{6,4},{7,5},{8,10},{9,11},{10,... | collective-permute-start | bytes 98312 | tf_op jit(solution)/shard_map/ppermute | solution.py:216
  61.4 3.5 %collective-permute-start.13 = (f32[128,256]{1,0:T(8,128)S(1)}, f32[128,256]{1,0:T(8,128)S(1)}, u32[]{:S(2)}, u32[]{:S(2)}) collective-permute-start(f32[128,256]{1,0:T(8,128)S(1)} %pad_maximum_fusion.3), channel_id=1, source_target_pairs={{0,1},{1,0},{2,3},{3,2},{4,5},{5,4},{6,7},{7,6},{8,9},{9,8},{10,11... | collective-permute-start | bytes 393224 | tf_op jit(solution)/shard_map/ppermute | solution.py:216
  64.1 1.9 %collective-permute-start.24 = (f32[128,256]{1,0:T(8,128)S(1)}, f32[128,256]{1,0:T(8,128)S(1)}, u32[]{:S(2)}, u32[]{:S(2)}) collective-permute-start(f32[128,256]{1,0:T(8,128)S(1)} %pad_maximum_fusion.4.own_ref), channel_id=1, source_target_pairs={{0,1},{1,0},{2,3},{3,2},{4,5},{5,4},{6,7},{7,6},{8,9},{9,8},{10,11... | collective-permute-start | bytes 393224 | tf_op jit(solution)/shard_map/ppermute | solution.py:216
